TPU v7x, 32 devices: a whole 2x2x4 slice. The times are simulated.
32 devices in a mesh: row: 8 (over y, x, core), col: 4 (over z).
Axes of the slice: x: 2, y: 2, z: 4, core: 2. Of those that a mesh axis runs over, the one named last changes fastest.
Arguments:
- start_vectors: bfloat16 [16384, 128], P(('row', 'col')), may hold values from -6 to 6
- tiles: bfloat16 [8, 128, 128, 128], P('row', 'col'), may hold values from -0.09375 to 0.09375
- tile_rows: int32 [8, 128], P('row', 'col'), may hold values from 0 to 15, as said below
- tile_cols: int32 [8, 128], P('row', 'col'), may hold values from 0 to 19
- tile_counts: int32 [8, 4], P('row', 'col'), may hold values from 4 to 32, as said below
- center: float32 [1], replicated, may hold values from -1 to 1
- half_width: float32 [1], replicated, may hold values from 2 to 3
Outputs:
- filtered: bfloat16 [16384, 128], P(('row', 'col'))
Inputs may be any that keep to these rules, and one draw needn't show every extreme that they name: On each device the 32 slots name different places (tile_rows, tile_cols); only the first tile_counts slots are in use. `tile_counts`: some device uses exactly 32 slots.
All inputs are finite; a program needn't handle non-finite values.
Results may differ from a plain program's by a relative error of at most 0.009.
Values may be sent and summed in bfloat16 or wider, within the bound.
A program may use at most 64 MiB of HBM per device.

v0:
```python
from functools import partial

import jax
import jax.numpy as jnp
from jax import lax
from jax.sharding import PartitionSpec as P


def passed_along(x, axis, by):
    peers = lax.axis_size(axis)
    return lax.ppermute(x, axis, [(i, (i + by) % peers) for i in range(peers)])


def collect_window(own_piece, levels, half_axis):
    stacked = own_piece[None]
    for section_index in range(levels + 1):
        if section_index < levels:
            distance = 1 << section_index
            source = stacked
        else:
            distance = half_axis
            source = own_piece[None]
        received = passed_along(source, "row", -distance)
        stacked = jnp.concatenate([stacked, received], axis=0)
    return stacked


def return_partials(partials, levels, half_axis):
    gathered = partials[:half_axis]
    for section_index in range(levels + 1):
        if section_index == 0:
            distance = half_axis
            source = partials[half_axis:]
        else:
            distance = 1 << levels - section_index
            source = gathered[distance : 2 * distance]
        received = passed_along(source.astype(jnp.bfloat16), "row", distance).astype(source.dtype)
        if section_index == 0:
            gathered = jnp.concatenate([gathered[:1] + received, gathered[1:]], axis=0)
        else:
            gathered = gathered[:distance] + received
    return gathered[0]


def direct_rows(row_select, tile_size, vec_count, products, row_start, row_count):
    summed = jnp.einsum("it,tan->ian", row_select, products, precision=lax.Precision.HIGHEST)
    return summed.reshape(row_count, vec_count)


def per_device(start_vectors, tiles, tile_rows, tile_cols, tile_counts, center, half_width):
    row_devices = lax.axis_size("row")
    col_devices = lax.axis_size("col")
    half_axis = row_devices // 2
    levels = half_axis.bit_length() - 1
    blocks = half_axis + 1
    piece_rows, vec_count = start_vectors.shape
    tile_size = tiles.shape[-1]
    slot_count = tiles.shape[1]
    piece_tiles = piece_rows // tile_size
    segment_rows = piece_rows * col_devices
    row_tiles = segment_rows // tile_size
    my_tiles = tiles[0]
    rows_list = tile_rows[0]
    cols_list = tile_cols[0]
    in_use = jnp.arange(slot_count, dtype=jnp.int32) < tile_counts[0, 0]
    row_select = (
        (rows_list[None, :] == jnp.arange(row_tiles, dtype=jnp.int32)[:, None]) & in_use[None, :]
    ).astype(jnp.float32)
    col_select = (
        (cols_list[None, :] == jnp.arange(blocks * piece_tiles, dtype=jnp.int32)[:, None])
        & in_use[None, :]
    ).astype(jnp.float32)
    shift_value = center[0]
    width_value = half_width[0]
    row_fn = partial(direct_rows, row_select, tile_size, vec_count)

    def direct_terms(own_piece):
        window = collect_window(own_piece, levels, half_axis)
        inputs = window.reshape(blocks * piece_tiles, tile_size, vec_count)[cols_list]
        return jnp.einsum("tab,tbn->tan", my_tiles, inputs, preferred_element_type=jnp.float32)

    def transposed_piece(whole_segment):
        inputs = whole_segment.reshape(row_tiles, tile_size, vec_count)[rows_list]
        products = jnp.einsum("tab,tan->tbn", my_tiles, inputs, preferred_element_type=jnp.float32)
        partials = jnp.einsum("jt,tbn->jbn", col_select, products, precision=lax.Precision.HIGHEST)
        return return_partials(partials.reshape(blocks, piece_rows, vec_count), levels, half_axis)

    def both_products(own_piece, whole_segment):
        products = direct_terms(own_piece)
        back_piece = transposed_piece(whole_segment)
        return (products, back_piece)

    def gather_vectors(vector_piece):
        return lax.all_gather(vector_piece, "col", axis=0, tiled=True)

    def summed_direct(products):
        return lax.psum_scatter(
            row_fn(products, jnp.int32(0), piece_rows * lax.axis_size("col")),
            "col",
            scatter_dimension=0,
            tiled=True,
        )

    start_float = start_vectors.astype(jnp.float32)
    whole_start = gather_vectors(start_vectors)
    products, back_piece = both_products(start_vectors, whole_start)
    applied = summed_direct(products) + back_piece
    first_piece = ((applied - shift_value * start_float) / width_value).astype(jnp.bfloat16)
    first_whole = gather_vectors(first_piece)
    products, back_piece = both_products(first_piece, first_whole)
    applied = summed_direct(products) + back_piece
    result = (
        2.0 * (applied - shift_value * first_piece.astype(jnp.float32)) / width_value - start_float
    )
    return result.astype(jnp.bfloat16)


def solution(mesh):
    return jax.shard_map(
        per_device,
        mesh=mesh,
        in_specs=(
            P(("row", "col"), None),
            P("row", "col", None, None),
            P("row", "col"),
            P("row", "col"),
            P("row", "col"),
            P(),
            P(),
        ),
        out_specs=P(("row", "col"), None),
        check_vma=False,
    )
```

profile of v0, /device:TPU:0, one launch (start us, length us, event | category | flops | bytes accessed | tf_op | source)
XLA Modules:
  0.0 147.3 jit_solution(6395739492037378806)
XLA Ops:
  6.5 3.4 %collective-permute-start = (bf16[1,512,128]{2,1,0:T(8,128)(2,1)}, bf16[1,512,128]{2,1,0:T(8,128)(2,1)S(1)}, u32[]{:S(2)}, u32[]{:S(2)}) collective-permute-start(bf16[1,512,128]{2,1,0:T(8,128)(2,1)} %bitcast.103), channel_id=1, source_target_pairs={{0,28},{4,0},{8,4},{12,8},{16,12},{20,16},{24,20},{28,24},{1,29},{... | collective-permute-start | bytes 393224 | tf_op jit(solution)/shard_map/ppermute | solution.py:11
  10.4 2.3 %collective-permute-done = bf16[1,512,128]{2,1,0:T(8,128)(2,1)S(1)} collective-permute-done((bf16[1,512,128]{2,1,0:T(8,128)(2,1)}, bf16[1,512,128]{2,1,0:T(8,128)(2,1)S(1)}, u32[]{:S(2)}, u32[]{:S(2)}) %collective-permute-start) | collective-permute-done | bytes 131104 | tf_op jit(solution)/shard_map/ppermute | solution.py:11
  15.6 6.8 %collective-permute-done.1 = bf16[2,512,128]{2,1,0:T(8,128)(2,1)S(1)} collective-permute-done((bf16[2,512,128]{2,1,0:T(8,128)(2,1)S(1)}, bf16[2,512,128]{2,1,0:T(8,128)(2,1)S(1)}, u32[]{:S(2)}, u32[]{:S(2)}) %collective-permute-start.1) | collective-permute-done | bytes 262176 | tf_op jit(solution)/shard_map/ppermute | solution.py:11
  23.4 1.7 %gather_fusion = bf16[32,128,128]{2,1,0:T(8,128)(2,1)} fusion(bf16[20,128,128]{2,1,0:T(8,128)(2,1)S(1)} %bitcast.100, s32[1024]{0:T(1024)S(1)} %pad_clamp_fusion.1), kind=kCustom, calls=%fused_computation | custom fusion | bytes 2097280 | tf_op jit(solution)/shard_map/gather | solution.py:79
  25.1 2.1 %fusion.14 = f32[32,128,128]{2,1,0:T(8,128)S(1)} fusion(bf16[32,128,128]{2,1,0:T(8,128)(2,1)} %gather_fusion, bf16[1,32,128,128]{3,2,1,0:T(8,128)(2,1)S(1)} %copy-done), kind=kOutput, calls=%fused_computation.18 | convolution fusion | flops 134217728 | bytes 4194304 | tf_op jit(solution)/shard_map/tab,tbn->tan/dot_general | solution.py:80
  27.2 2.1 %copy.18 = f32[32,128,128]{1,0,2:T(8,128)} copy(f32[32,128,128]{2,1,0:T(8,128)S(1)} %fusion.14) | data formatting | bytes 4194304 | tf_op jit(solution)/shard_map/tab,tbn->tan/dot_general | solution.py:80
  29.2 2.4 %fusion.6 = f32[16,128,128]{2,0,1:T(8,128)S(1)} fusion(f32[32,128,128]{1,0,2:T(8,128)} %copy.18, s32[32]{0:T(128)S(1)} %bitcast.119, pred[32]{0:T(512)(128)(4,1)S(1)} %iota_compare_fusion.2), kind=kOutput, calls=%fused_computation.10 | convolution fusion | flops 100664320 | bytes 3145888 | tf_op jit(solution)/shard_map/it,tan->ian/dot_general | solution.py:46
  31.6 1.3 copy.8
  33.0 22.3 %all_gather.6 = bf16[2048,128]{1,0:T(8,128)(2,1)S(1)} all-gather(bf16[512,128]{1,0:T(8,128)(2,1)S(1)} %copy-done.1), channel_id=1, replica_groups=mesh['row'=8,'col'=4] {'col'}, dimensions={0}, use_global_device_ids=true | all-gather | bytes 655360 | tf_op jit(solution)/shard_map/all_gather | solution.py:94
  56.1 1.9 %fusion.12 = f32[32,128,128]{2,1,0:T(8,128)} fusion(bf16[32,128,128]{2,1,0:T(8,128)(2,1)S(1)} %gather_fusion.1, bf16[1,32,128,128]{3,2,1,0:T(8,128)(2,1)S(1)} %copy-done), kind=kOutput, calls=%fused_computation.16 | convolution fusion | flops 134217728 | bytes 4194304 | tf_op jit(solution)/shard_map/tab,tan->tbn/dot_general | solution.py:84
  58.0 2.4 %copy.19 = f32[32,128,128]{1,0,2:T(8,128)S(1)} copy(f32[32,128,128]{2,1,0:T(8,128)} %fusion.12) | data formatting | bytes 4194304 | tf_op jit(solution)/shard_map/tab,tan->tbn/dot_general | solution.py:84
  60.4 1.0 fusion.47
  62.2 7.7 %collective-permute-done.3 = bf16[1,512,128]{2,1,0:T(8,128)(2,1)S(1)} collective-permute-done((bf16[1,512,128]{2,1,0:T(8,128)(2,1)S(1)}, bf16[1,512,128]{2,1,0:T(8,128)(2,1)S(1)}, u32[]{:S(2)}, u32[]{:S(2)}) %collective-permute-start.3) | collective-permute-done | bytes 131104 | tf_op jit(solution)/shard_map/ppermute | solution.py:11
  71.4 4.0 %collective-permute-done.5 = bf16[1,512,128]{2,1,0:T(8,128)(2,1)S(1)} collective-permute-done((bf16[1,512,128]{2,1,0:T(8,128)(2,1)S(1)}, bf16[1,512,128]{2,1,0:T(8,128)(2,1)S(1)}, u32[]{:S(2)}, u32[]{:S(2)}) %collective-permute-start.5) | collective-permute-done | bytes 131104 | tf_op jit(solution)/shard_map/ppermute | solution.py:11
  75.4 1.0 fusion.20
  76.5 2.5 %collective-permute-done.6 = bf16[1,512,128]{2,1,0:T(8,128)(2,1)S(1)} collective-permute-done((bf16[1,512,128]{2,1,0:T(8,128)(2,1)S(1)}, bf16[1,512,128]{2,1,0:T(8,128)(2,1)S(1)}, u32[]{:S(2)}, u32[]{:S(2)}) %collective-permute-start.6) | collective-permute-done | bytes 131104 | tf_op jit(solution)/shard_map/ppermute | solution.py:11
  79.1 1.1 collective-permute-start.8
  80.2 3.9 %collective-permute-done.8 = bf16[1,512,128]{2,1,0:T(8,128)(2,1)S(1)} collective-permute-done((bf16[1,512,128]{2,1,0:T(8,128)(2,1)S(1)}, bf16[1,512,128]{2,1,0:T(8,128)(2,1)S(1)}, u32[]{:S(2)}, u32[]{:S(2)}) %collective-permute-start.8) | collective-permute-done | bytes 131104 | tf_op jit(solution)/shard_map/ppermute | solution.py:11
  84.1 4.1 %collective-permute-done.7 = bf16[2,512,128]{2,1,0:T(8,128)(2,1)S(1)} collective-permute-done((bf16[2,512,128]{2,1,0:T(8,128)(2,1)S(1)}, bf16[2,512,128]{2,1,0:T(8,128)(2,1)S(1)}, u32[]{:S(2)}, u32[]{:S(2)}) %collective-permute-start.7) | collective-permute-done | bytes 262176 | tf_op jit(solution)/shard_map/ppermute | solution.py:11
  88.3 1.7 %gather_fusion.2 = bf16[32,128,128]{2,1,0:T(8,128)(2,1)} fusion(bf16[20,128,128]{2,1,0:T(8,128)(2,1)S(1)} %bitcast.99, s32[1024]{0:T(1024)S(1)} %pad_clamp_fusion.1), kind=kCustom, calls=%fused_computation.2 | custom fusion | bytes 2097280 | tf_op jit(solution)/shard_map/gather | solution.py:79
  89.9 2.1 %fusion.10 = f32[32,128,128]{2,1,0:T(8,128)S(1)} fusion(bf16[32,128,128]{2,1,0:T(8,128)(2,1)} %gather_fusion.2, bf16[1,32,128,128]{3,2,1,0:T(8,128)(2,1)S(1)} %copy-done), kind=kOutput, calls=%fused_computation.14 | convolution fusion | flops 134217728 | bytes 4194304 | tf_op jit(solution)/shard_map/tab,tbn->tan/dot_general | solution.py:80
  92.0 2.1 %copy.20 = f32[32,128,128]{1,0,2:T(8,128)} copy(f32[32,128,128]{2,1,0:T(8,128)S(1)} %fusion.10) | data formatting | bytes 4194304 | tf_op jit(solution)/shard_map/tab,tbn->tan/dot_general | solution.py:80
  94.1 2.4 %fusion.2 = f32[16,128,128]{2,0,1:T(8,128)S(1)} fusion(f32[32,128,128]{1,0,2:T(8,128)} %copy.20, s32[32]{0:T(128)S(1)} %bitcast.120, pred[32]{0:T(512)(128)(4,1)S(1)} %iota_compare_fusion.2), kind=kOutput, calls=%fused_computation.6 | convolution fusion | flops 100664320 | bytes 3145888 | tf_op jit(solution)/shard_map/it,tan->ian/dot_general | solution.py:46
  96.5 1.3 copy.13
  97.8 19.3 %all_gather.7 = bf16[2048,128]{1,0:T(8,128)(2,1)S(1)} all-gather(bf16[512,128]{1,0:T(8,128)(2,1)S(1)} %fusion.20), channel_id=1, replica_groups=mesh['row'=8,'col'=4] {'col'}, dimensions={0}, use_global_device_ids=true | all-gather | bytes 655360 | tf_op jit(solution)/shard_map/all_gather | solution.py:94
  117.9 1.9 %fusion.8 = f32[32,128,128]{2,1,0:T(8,128)} fusion(bf16[32,128,128]{2,1,0:T(8,128)(2,1)S(1)} %gather_fusion.3, bf16[1,32,128,128]{3,2,1,0:T(8,128)(2,1)S(1)} %copy-done), kind=kOutput, calls=%fused_computation.12 | convolution fusion | flops 134217728 | bytes 4194304 | tf_op jit(solution)/shard_map/tab,tan->tbn/dot_general | solution.py:84
  119.7 2.4 %copy.21 = f32[32,128,128]{1,0,2:T(8,128)S(1)} copy(f32[32,128,128]{2,1,0:T(8,128)} %fusion.8) | data formatting | bytes 4194304 | tf_op jit(solution)/shard_map/tab,tan->tbn/dot_general | solution.py:84
  123.6 4.6 %collective-permute-start.10 = (bf16[2,512,128]{2,1,0:T(8,128)(2,1)S(1)}, bf16[2,512,128]{2,1,0:T(8,128)(2,1)S(1)}, u32[]{:S(2)}, u32[]{:S(2)}) collective-permute-start(bf16[2,512,128]{2,1,0:T(8,128)(2,1)S(1)} %bitcast.116), channel_id=1, source_target_pairs={{0,8},{4,12},{8,16},{12,20},{16,24},{20,28},{24,0},{28,4},{1,9},{5... | collective-permute-start | bytes 786440 | tf_op jit(solution)/shard_map/ppermute | solution.py:11
  128.6 2.0 %collective-permute-done.9 = bf16[1,512,128]{2,1,0:T(8,128)(2,1)S(1)} collective-permute-done((bf16[1,512,128]{2,1,0:T(8,128)(2,1)S(1)}, bf16[1,512,128]{2,1,0:T(8,128)(2,1)S(1)}, u32[]{:S(2)}, u32[]{:S(2)}) %collective-permute-start.9) | collective-permute-done | bytes 131104 | tf_op jit(solution)/shard_map/ppermute | solution.py:11
  130.6 2.8 %collective-permute-done.10 = bf16[2,512,128]{2,1,0:T(8,128)(2,1)S(1)} collective-permute-done((bf16[2,512,128]{2,1,0:T(8,128)(2,1)S(1)}, bf16[2,512,128]{2,1,0:T(8,128)(2,1)S(1)}, u32[]{:S(2)}, u32[]{:S(2)}) %collective-permute-start.10) | collective-permute-done | bytes 262176 | tf_op jit(solution)/shard_map/ppermute | solution.py:11
  133.5 5.3 %collective-permute-done.11 = bf16[1,512,128]{2,1,0:T(8,128)(2,1)S(1)} collective-permute-done((bf16[1,512,128]{2,1,0:T(8,128)(2,1)S(1)}, bf16[1,512,128]{2,1,0:T(8,128)(2,1)S(1)}, u32[]{:S(2)}, u32[]{:S(2)}) %collective-permute-start.11) | collective-permute-done | bytes 131104 | tf_op jit(solution)/shard_map/ppermute | solution.py:11
  138.8 1.7 %fusion.21 = bf16[512,128]{1,0:T(8,128)(2,1)} fusion(bf16[512,128]{1,0:T(8,128)(2,1)S(1)} %copy-done.1, f32[512,128]{1,0:T(8,128)} %reduce-scatter.5.cloned.1.call-done, f32[2,512,128]{2,1,0:T(8,128)S(1)} %fusion.16, bf16[512,128]{1,0:T(8,128)(2,1)S(1)} %fusion.20, bf16[1,512,128]{2,1,0:T(8,128)(2,1)S(1)} %collective-permute-done.11, f32[]{:T(128)} %bitcast.96, ...), kind=kLoop, calls=%fused_computation.31 | loop fusion | flops 720896 | bytes 1048584 | tf_op jit(solution)/shard_map/convert_element_type | solution.py:115
  (59 shorter events, 8.3 us)
Async XLA Ops:
  6.5 18.5 %copy-start = (bf16[1,32,128,128]{3,2,1,0:T(8,128)(2,1)S(1)}, bf16[1,32,128,128]{3,2,1,0:T(8,128)(2,1)}, u32[]{:S(2)}) copy-start(bf16[1,32,128,128]{3,2,1,0:T(8,128)(2,1)} %param.8) | copy-start | bytes 3145732
  6.5 68.8 %reduce-scatter.3.cloned.1.call-start = ((), (), s32[]{:S(2)}) async-start(), calls=%async_computation.2 | async-start | bytes 1310720 | tf_op jit(solution)/shard_map/reduce_scatter | solution.py:97
  6.5 6.2 %collective-permute-start = (bf16[1,512,128]{2,1,0:T(8,128)(2,1)}, bf16[1,512,128]{2,1,0:T(8,128)(2,1)S(1)}, u32[]{:S(2)}, u32[]{:S(2)}) collective-permute-start(bf16[1,512,128]{2,1,0:T(8,128)(2,1)} %bitcast.103), channel_id=1, source_target_pairs={{0,28},{4,0},{8,4},{12,8},{16,12},{20,16},{24,20},{28,24},{1,29},{... | collective-permute-start | bytes 393224 | tf_op jit(solution)/shard_map/ppermute | solution.py:11
  9.9 5.7 %collective-permute-start.2 = (bf16[1,512,128]{2,1,0:T(8,128)(2,1)}, bf16[1,512,128]{2,1,0:T(8,128)(2,1)S(1)}, u32[]{:S(2)}, u32[]{:S(2)}) collective-permute-start(bf16[1,512,128]{2,1,0:T(8,128)(2,1)} %bitcast.104), channel_id=1, source_target_pairs={{0,16},{4,20},{8,24},{12,28},{16,0},{20,4},{24,8},{28,12},{1,17},{... | collective-permute-start | bytes 393224 | tf_op jit(solution)/shard_map/ppermute | solution.py:11
  13.7 8.7 %collective-permute-start.1 = (bf16[2,512,128]{2,1,0:T(8,128)(2,1)S(1)}, bf16[2,512,128]{2,1,0:T(8,128)(2,1)S(1)}, u32[]{:S(2)}, u32[]{:S(2)}) collective-permute-start(bf16[2,512,128]{2,1,0:T(8,128)(2,1)S(1)} %pad_maximum_fusion.4), channel_id=1, source_target_pairs={{0,24},{4,28},{8,0},{12,4},{16,8},{20,12},{24,16},{28,20},{1,25},{... | collective-permute-start | bytes 786440 | tf_op jit(solution)/shard_map/ppermute | solution.py:11
  27.2 2.1 %copy-start.2 = (s32[1,32]{1,0:T(1,128)S(1)}, s32[1,32]{1,0:T(1,128)}, u32[]{:S(2)}) copy-start(s32[1,32]{1,0:T(1,128)} %param.9) | copy-start | bytes 388
  31.6 1.4 copy-start.1
  33.0 105.8 %reduce-scatter.5.cloned.1.call-start = ((), (), s32[]{:S(2)}) async-start(), calls=%async_computation.3 | async-start | bytes 1310720 | tf_op jit(solution)/shard_map/reduce_scatter | solution.py:97
  58.0 2.4 %copy-start.3 = (s32[1,32]{1,0:T(1,128)S(1)}, s32[1,32]{1,0:T(1,128)}, u32[]{:S(2)}) copy-start(s32[1,32]{1,0:T(1,128)} %param.10) | copy-start | bytes 388
  61.5 8.4 %collective-permute-start.3 = (bf16[1,512,128]{2,1,0:T(8,128)(2,1)S(1)}, bf16[1,512,128]{2,1,0:T(8,128)(2,1)S(1)}, u32[]{:S(2)}, u32[]{:S(2)}) collective-permute-start(bf16[1,512,128]{2,1,0:T(8,128)(2,1)S(1)} %bitcast.117), channel_id=1, source_target_pairs={{0,16},{4,20},{8,24},{12,28},{16,0},{20,4},{24,8},{28,12},{1,17},{... | collective-permute-start | bytes 393224 | tf_op jit(solution)/shard_map/ppermute | solution.py:11
  61.7 8.3 %collective-permute-start.4 = (bf16[2,512,128]{2,1,0:T(8,128)(2,1)S(1)}, bf16[2,512,128]{2,1,0:T(8,128)(2,1)S(1)}, u32[]{:S(2)}, u32[]{:S(2)}) collective-permute-start(bf16[2,512,128]{2,1,0:T(8,128)(2,1)S(1)} %bitcast.115), channel_id=1, source_target_pairs={{0,8},{4,12},{8,16},{12,20},{16,24},{20,28},{24,0},{28,4},{1,9},{5... | collective-permute-start | bytes 786440 | tf_op jit(solution)/shard_map/ppermute | solution.py:11
  70.0 5.3 %collective-permute-start.5 = (bf16[1,512,128]{2,1,0:T(8,128)(2,1)S(1)}, bf16[1,512,128]{2,1,0:T(8,128)(2,1)S(1)}, u32[]{:S(2)}, u32[]{:S(2)}) collective-permute-start(bf16[1,512,128]{2,1,0:T(8,128)(2,1)S(1)} %slice.135), channel_id=1, source_target_pairs={{0,4},{4,8},{8,12},{12,16},{16,20},{20,24},{24,28},{28,0},{1,5},{5... | collective-permute-start | bytes 393224 | tf_op jit(solution)/shard_map/ppermute | solution.py:11
  76.4 2.6 %collective-permute-start.6 = (bf16[1,512,128]{2,1,0:T(8,128)(2,1)S(1)}, bf16[1,512,128]{2,1,0:T(8,128)(2,1)S(1)}, u32[]{:S(2)}, u32[]{:S(2)}) collective-permute-start(bf16[1,512,128]{2,1,0:T(8,128)(2,1)S(1)} %bitcast.107), channel_id=1, source_target_pairs={{0,28},{4,0},{8,4},{12,8},{16,12},{20,16},{24,20},{28,24},{1,29},{... | collective-permute-start | bytes 393224 | tf_op jit(solution)/shard_map/ppermute | solution.py:11
  79.0 9.2 %collective-permute-start.7 = (bf16[2,512,128]{2,1,0:T(8,128)(2,1)S(1)}, bf16[2,512,128]{2,1,0:T(8,128)(2,1)S(1)}, u32[]{:S(2)}, u32[]{:S(2)}) collective-permute-start(bf16[2,512,128]{2,1,0:T(8,128)(2,1)S(1)} %pad_maximum_fusion.5), channel_id=1, source_target_pairs={{0,24},{4,28},{8,0},{12,4},{16,8},{20,12},{24,16},{28,20},{1,25},{... | collective-permute-start | bytes 786440 | tf_op jit(solution)/shard_map/ppermute | solution.py:11
  79.1 5.0 %collective-permute-start.8 = (bf16[1,512,128]{2,1,0:T(8,128)(2,1)S(1)}, bf16[1,512,128]{2,1,0:T(8,128)(2,1)S(1)}, u32[]{:S(2)}, u32[]{:S(2)}) collective-permute-start(bf16[1,512,128]{2,1,0:T(8,128)(2,1)S(1)} %bitcast.109), channel_id=1, source_target_pairs={{0,16},{4,20},{8,24},{12,28},{16,0},{20,4},{24,8},{28,12},{1,17},{... | collective-permute-start | bytes 393224 | tf_op jit(solution)/shard_map/ppermute | solution.py:11
  123.2 7.4 %collective-permute-start.9 = (bf16[1,512,128]{2,1,0:T(8,128)(2,1)S(1)}, bf16[1,512,128]{2,1,0:T(8,128)(2,1)S(1)}, u32[]{:S(2)}, u32[]{:S(2)}) collective-permute-start(bf16[1,512,128]{2,1,0:T(8,128)(2,1)S(1)} %bitcast.118), channel_id=1, source_target_pairs={{0,16},{4,20},{8,24},{12,28},{16,0},{20,4},{24,8},{28,12},{1,17},{... | collective-permute-start | bytes 393224 | tf_op jit(solution)/shard_map/ppermute | solution.py:11
  123.6 9.8 %collective-permute-start.10 = (bf16[2,512,128]{2,1,0:T(8,128)(2,1)S(1)}, bf16[2,512,128]{2,1,0:T(8,128)(2,1)S(1)}, u32[]{:S(2)}, u32[]{:S(2)}) collective-permute-start(bf16[2,512,128]{2,1,0:T(8,128)(2,1)S(1)} %bitcast.116), channel_id=1, source_target_pairs={{0,8},{4,12},{8,16},{12,20},{16,24},{20,28},{24,0},{28,4},{1,9},{5... | collective-permute-start | bytes 786440 | tf_op jit(solution)/shard_map/ppermute | solution.py:11
  133.5 5.3 %collective-permute-start.11 = (bf16[1,512,128]{2,1,0:T(8,128)(2,1)S(1)}, bf16[1,512,128]{2,1,0:T(8,128)(2,1)S(1)}, u32[]{:S(2)}, u32[]{:S(2)}) collective-permute-start(bf16[1,512,128]{2,1,0:T(8,128)(2,1)S(1)} %slice.134), channel_id=1, source_target_pairs={{0,4},{4,8},{8,12},{12,16},{16,20},{20,24},{24,28},{28,0},{1,5},{5... | collective-permute-start | bytes 393224 | tf_op jit(solution)/shard_map/ppermute | solution.py:11
Sparse Core Ops, SparseCore 0:
  33.1 32.1 reduce-scatter.2
  97.9 32.0 reduce-scatter.4
where the time goes:
time: 148 us; the launch traced here: 147 us
  blocking collectives  41.6 us (28%)
  waiting for transfers between devices  41.4 us (28%)
  local copies, waits for them, and re-layouts  17.4 us (12%)
  between operations  15.7 us (11%)
  matrix products  14.7 us (10%)
  starting transfers between devices  10.9 us (7%)
  other arithmetic  5.56 us (4%)
    all_gather x2, blocking collectives, gather_vectors(): return lax.all_gather(vector_piece, 'col', axis=0, tiled=True)  41.6 us
    ppermute x12, waiting for transfers between devices, passed_along(): return lax.ppermute(x, axis, [(i, (i + by) % peers) for i in range(peers)])  41.4 us
    ppermute x12, starting transfers between devices, passed_along(): return lax.ppermute(x, axis, [(i, (i + by) % peers) for i in range(peers)])  10.8 us
    dot_general x2, matrix products, direct_rows(): jnp.einsum('it,tan->ian', row_select, products, precision=lax.Precision.H...  4.78 us
    dot_general x2, local copies, waits for them, and re-layouts, transposed_piece(): jnp.einsum('tab,tan->tbn', my_tiles, inputs, preferred_element_type=jnp.f...  4.77 us
    dot_general x2, matrix products, direct_terms(): jnp.einsum('tab,tbn->tan', my_tiles, inputs, preferred_element_type=jnp.f...  4.2 us
    dot_general x2, local copies, waits for them, and re-layouts, direct_terms(): jnp.einsum('tab,tbn->tan', my_tiles, inputs, preferred_element_type=jnp.f...  4.14 us
    dot_general x2, matrix products, transposed_piece(): jnp.einsum('tab,tan->tbn', my_tiles, inputs, preferred_element_type=jnp.f...  3.72 us
  transfers between devices with their start and end apart: 14, of which 10 were waited for; matrix products, arithmetic and copies ran while one was open for 10% of the time, Pallas kernels for 0%

commit v1 on v0

v1 whole, which is shorter than its diff:
```python
import functools

import jax
import jax.numpy as jnp
from jax import lax
from jax.experimental import pallas as pl
from jax.experimental.pallas import tpu as pltpu
from jax.sharding import PartitionSpec as P

CHUNKS = 2
UNROLL = 8
MESH_ID = pl.DeviceIdType.MESH


def link_slots(rows_ref, cols_ref, counts_ref, prev_ref, last_ref, *, slots, row_tiles, col_tiles):
    for side, (keys, size) in enumerate(((rows_ref, row_tiles), (cols_ref, col_tiles))):
        for k in range(size):
            last_ref[side, k] = slots
        for s in range(slots):
            key = keys[0, s]
            used = s < counts_ref[0, 0]
            before = last_ref[side, key]
            prev_ref[side, s] = jnp.where(used, before, slots)
            last_ref[side, key] = jnp.where(used, s, before)


def filter_kernel(
    dims, x_ref, tiles_ref, rows_ref, cols_ref, prev_ref, last_ref, center_ref, width_ref,
    out_ref, *scratch,
):
    R, C, half, pt, slots, vec, size = dims
    vc = vec // CHUNKS
    it = iter(scratch)
    win = [[next(it) for _ in range(CHUNKS)] for _ in range(2)]
    seg = [[next(it) for _ in range(CHUNKS)] for _ in range(2)]
    row_out = [[next(it) for _ in range(CHUNKS)] for _ in range(2)]
    col_out = [[next(it) for _ in range(CHUNKS)] for _ in range(2)]
    row_in = [[next(it) for _ in range(CHUNKS)] for _ in range(2)]
    col_in = [[next(it) for _ in range(CHUNKS)] for _ in range(2)]
    back = [next(it) for _ in range(CHUNKS)]
    direct = [next(it) for _ in range(CHUNKS)]
    result = next(it)
    row_send, row_recv, col_send, col_recv = (next(it) for _ in range(4))

    r = lax.axis_index("row")
    c = lax.axis_index("col")

    row_offsets = sorted({b % R for b in range(1, half + 1)} | {-b % R for b in range(1, half + 1)})
    barrier = pltpu.get_barrier_semaphore()
    for off in row_offsets:
        pl.semaphore_signal(barrier, inc=1, device_id={"row": lax.rem(r + off, R)}, device_id_type=MESH_ID)
    for off in range(1, C):
        pl.semaphore_signal(barrier, inc=1, device_id={"col": lax.rem(c + off, C)}, device_id_type=MESH_ID)

    for j in range(pt):
        block = x_ref[j * size:(j + 1) * size, :].astype(jnp.float32).T.astype(jnp.bfloat16)
        for h in range(CHUNKS):
            part = block[h * vc:(h + 1) * vc, :]
            win[0][h][j] = part
            seg[0][h][c * pt + j] = part
    for h in range(CHUNKS):
        back[h][slots] = jnp.zeros((vc, size), jnp.float32)
        direct[h][slots] = jnp.zeros((vc, size), jnp.float32)
    pl.semaphore_wait(barrier, len(row_offsets) + C - 1)

    def gather_copies(t, h):
        own = win[t][h].at[pl.ds(0, pt)]
        cols = [
            pltpu.make_async_remote_copy(
                src_ref=own, dst_ref=seg[t][h].at[pl.ds(c * pt, pt)],
                send_sem=col_send.at[t, h, 0, d], recv_sem=col_recv.at[t, h, 0, d],
                device_id={"col": lax.rem(c + d, C)}, device_id_type=MESH_ID)
            for d in range(1, C)
        ]
        rows = [
            pltpu.make_async_remote_copy(
                src_ref=own, dst_ref=win[t][h].at[pl.ds(b * pt, pt)],
                send_sem=row_send.at[t, h, 0, b], recv_sem=row_recv.at[t, h, 0, b],
                device_id={"row": lax.rem(r + R - b, R)}, device_id_type=MESH_ID)
            for b in range(1, half + 1)
        ]
        return cols, rows

    def row_returns(t, h):
        return [
            pltpu.make_async_remote_copy(
                src_ref=row_out[t][h].at[b - 1], dst_ref=row_in[t][h].at[b - 1],
                send_sem=row_send.at[t, h, 1, b], recv_sem=row_recv.at[t, h, 1, b],
                device_id={"row": lax.rem(r + b, R)}, device_id_type=MESH_ID)
            for b in range(1, half + 1)
        ]

    def col_returns(t, h):
        return [
            pltpu.make_async_remote_copy(
                src_ref=col_out[t][h].at[d - 1], dst_ref=col_in[t][h].at[d - 1],
                send_sem=col_send.at[t, h, 1, d], recv_sem=col_recv.at[t, h, 1, d],
                device_id={"col": lax.rem(c + d, C)}, device_id_type=MESH_ID)
            for d in range(1, C)
        ]

    started = []

    def start_all(copies):
        for copy in copies:
            copy.start()
        started.extend(copies)
        return copies

    def products(source, index_ref, side, sums, transposed):
        contract = (((1,), (0,)), ((), ())) if transposed else (((1,), (1,)), ((), ()))

        def one(s, carry):
            term = lax.dot_general(
                source[index_ref[0, s]], tiles_ref[0, s], contract,
                preferred_element_type=jnp.float32)
            sums[s] = sums[prev_ref[side, s]] + term
            return carry

        lax.fori_loop(0, slots, one, 0, unroll=UNROLL)

    def compute(t, h, copies):
        cols, rows = copies
        for copy in cols:
            copy.wait_recv()
        products(seg[t][h], rows_ref, 1, back[h], True)
        for b in range(1, half + 1):
            for j in range(pt):
                row_out[t][h][b - 1, j] = back[h][last_ref[1, b * pt + j]].astype(jnp.bfloat16)
        returns = start_all(row_returns(t, h))
        for copy in rows:
            copy.wait_recv()
        products(win[t][h], cols_ref, 0, direct[h], False)
        for d in range(1, C):
            piece = lax.rem(c + d, C)
            for j in range(pt):
                col_out[t][h][d - 1, j] = direct[h][last_ref[0, piece * pt + j]].astype(jnp.bfloat16)
        return returns, start_all(col_returns(t, h))

    def applied(t, h, returns, j):
        total = back[h][last_ref[1, j]] + direct[h][last_ref[0, c * pt + j]]
        for b in range(half):
            total += row_in[t][h][b, j].astype(jnp.float32)
        for d in range(C - 1):
            total += col_in[t][h][d, j].astype(jnp.float32)
        return total

    shift = center_ref[0]
    width = width_ref[0]
    gathers = [None] * CHUNKS
    for h in range(CHUNKS):
        cols, rows = gather_copies(0, h)
        gathers[h] = (start_all(cols), start_all(rows))
    for t in range(2):
        returns = [compute(t, h, gathers[h]) for h in range(CHUNKS)]
        for h in range(CHUNKS):
            for group in returns[h]:
                for copy in group:
                    copy.wait_recv()
            for j in range(pt):
                begin = win[0][h][j].astype(jnp.float32)
                if t == 0:
                    first = ((applied(t, h, returns, j) - shift * begin) / width).astype(jnp.bfloat16)
                    win[1][h][j] = first
                    seg[1][h][c * pt + j] = first
                else:
                    first = win[1][h][j].astype(jnp.float32)
                    value = 2.0 * (applied(t, h, returns, j) - shift * first) / width - begin
                    result[j, h * vc:(h + 1) * vc, :] = value
            if t == 0:
                cols, rows = gather_copies(1, h)
                gathers[h] = (start_all(cols), start_all(rows))
    for j in range(pt):
        out_ref[j * size:(j + 1) * size, :] = result[j].T.astype(jnp.bfloat16)
    for copy in started:
        copy.wait_send()


def per_device(start_vectors, tiles, tile_rows, tile_cols, tile_counts, center, half_width):
    R = lax.axis_size("row")
    C = lax.axis_size("col")
    half = R // 2
    piece_rows, vec = start_vectors.shape
    size = tiles.shape[-1]
    slots = tiles.shape[1]
    pt = piece_rows // size
    vc = vec // CHUNKS
    row_tiles = pt * C
    col_tiles = pt * (half + 1)
    smem = pl.BlockSpec(memory_space=pltpu.SMEM)
    vmem = pl.BlockSpec(memory_space=pltpu.VMEM)
    prev, last = pl.pallas_call(
        functools.partial(link_slots, slots=slots, row_tiles=row_tiles, col_tiles=col_tiles),
        out_shape=(
            jax.ShapeDtypeStruct((2, slots), jnp.int32),
            jax.ShapeDtypeStruct((2, max(row_tiles, col_tiles)), jnp.int32),
        ),
        in_specs=[smem] * 3,
        out_specs=(smem, smem),
        name="link_slots",
    )(tile_rows, tile_cols, tile_counts)

    bf, f32 = jnp.bfloat16, jnp.float32

    def pair(shape, dtype):
        return [pltpu.VMEM(shape, dtype) for _ in range(2 * CHUNKS)]

    scratch = (
        pair((col_tiles, vc, size), bf)
        + pair((row_tiles, vc, size), bf)
        + pair((half, pt, vc, size), bf)
        + pair((C - 1, pt, vc, size), bf)
        + pair((half, pt, vc, size), bf)
        + pair((C - 1, pt, vc, size), bf)
        + [pltpu.VMEM((slots + 1, vc, size), f32) for _ in range(2 * CHUNKS)]
        + [pltpu.VMEM((pt, vec, size), f32)]
        + [pltpu.SemaphoreType.DMA((2, CHUNKS, 2, half + 1))] * 2
        + [pltpu.SemaphoreType.DMA((2, CHUNKS, 2, C))] * 2
    )
    return pl.pallas_call(
        functools.partial(filter_kernel, (R, C, half, pt, slots, vec, size)),
        out_shape=jax.ShapeDtypeStruct((piece_rows, vec), bf),
        in_specs=[vmem, vmem, smem, smem, smem, smem, smem, smem],
        out_specs=vmem,
        scratch_shapes=scratch,
        compiler_params=pltpu.CompilerParams(
            collective_id=0, has_side_effects=True, vmem_limit_bytes=40 << 20),
        name="filter_steps",
    )(start_vectors, tiles, tile_rows, tile_cols, prev, last, center, half_width)


def solution(mesh):
    return jax.shard_map(
        per_device,
        mesh=mesh,
        in_specs=(
            P(("row", "col"), None),
            P("row", "col", None, None),
            P("row", "col"),
            P("row", "col"),
            P("row", "col"),
            P(),
            P(),
        ),
        out_specs=P(("row", "col"), None),
        check_vma=False,
    )
```

time: 148 us -> 61 us (0.41)
  Pallas kernels: 0 us -> 55.3 us
  blocking collectives: 41.6 us -> 0 us
  waiting for transfers between devices: 41.4 us -> 0 us
  matrix products: 14.7 us -> 0 us
  local copies, waits for them, and re-layouts: 17.4 us -> 3.46 us
  between operations: 15.7 us -> 1.99 us
  starting transfers between devices: 10.9 us -> 0 us
  other arithmetic: 5.56 us -> 0 us
    pallas_call x0 -> x2, Pallas kernels: none -> 55.3 us  [the longest x1 53.8 us: per_device(): pl.pallas_call(functools.partial(filter_kernel, (R, C, half, pt, slots, v...]
    all_gather x2 -> x0, blocking collectives: 41.6 us -> none  [gather_vectors(): return lax.all_gather(vector_piece, 'col', axis=0, tiled=True)]
    ppermute x12 -> x0, waiting for transfers between devices: 41.4 us -> none  [passed_along(): return lax.ppermute(x, axis, [(i, (i + by) % peers) for i in range(peers)])]
    dot_general x8 -> x0, matrix products: 14.7 us -> none  [the longest x2 4.78 us: direct_rows(): jnp.einsum('it,tan->ian', row_select, products, precision=lax.Precision.H...]
    dot_general x6 -> x0, local copies, waits for them, and re-layouts: 11.5 us -> none  [the longest x2 4.77 us: transposed_piece(): jnp.einsum('tab,tan->tbn', my_tiles, inputs, preferred_element_type=jnp.f...]
    ppermute x12 -> x0, starting transfers between devices: 10.8 us -> none  [passed_along(): return lax.ppermute(x, axis, [(i, (i + by) % peers) for i in range(peers)])]
    gather x4 -> x0, local copies, waits for them, and re-layouts: 4.82 us -> none  [the longest x2 3.32 us: direct_terms(): window.reshape(blocks * piece_tiles, tile_size, vec_count)[cols_list]]
    unnamed x8 -> x13, local copies, waits for them, and re-layouts: 0.02 us -> 3.46 us
  transfers between devices with their start and end apart: 14 -> 0, of which waited for: 10 -> 0; matrix products, arithmetic and copies ran while one was open for 10% -> 0% of each run, Pallas kernels for 0% -> 0%
where the time goes in v1:
time: 61 us; the launch traced here: 60.8 us
  Pallas kernels  55.3 us (91%)
  local copies, waits for them, and re-layouts  3.46 us (6%)
  between operations  1.99 us (3%)
    pallas_call x1, Pallas kernels, per_device(): pl.pallas_call(functools.partial(filter_kernel, (R, C, half, pt, slots, v...  53.8 us
    unnamed x13, local copies, waits for them, and re-layouts  3.46 us
    pallas_call x1, Pallas kernels, per_device(): pl.pallas_call(functools.partial(link_slots, slots=slots, row_tiles=row_t...  1.55 us

profile of v1, /device:TPU:0, one launch (start us, length us, event | category | flops | bytes accessed | tf_op | source)
XLA Modules:
  0.0 60.8 jit_solution(4981073569438499082)
XLA Ops:
  1.9 1.6 %link_slots.1 = (s32[2,32]{1,0:T(2,128)}, s32[2,20]{1,0:T(2,128)}) custom-call(s32[1,32]{1,0:T(1,128)} %rows_ref.3, s32[1,32]{1,0:T(1,128)} %cols_ref.3, s32[1,1]{1,0:T(1,128)S(6)} %copy.9.counts_ref), custom_call_target="tpu_custom_call" | custom-call | tf_op jit(solution)/shard_map/link_slots/pallas_call | solution.py:192
  3.5 0.0 copy-start.3
  3.5 0.0 copy-start.5
  3.5 0.0 copy-start.2
  3.5 0.0 copy-start.4
  3.5 0.6 %copy-done.3 = s32[2,20]{1,0:T(2,128)S(1)} copy-done((s32[2,20]{1,0:T(2,128)S(1)}, s32[2,20]{1,0:T(2,128)}, u32[]{:S(2)}) %copy-start.3) | copy-done | bytes 184
  4.2 0.0 copy-done.5
  4.2 0.0 copy-done.2
  4.2 0.0 copy-done.4
  4.2 0.0 copy-start
  4.2 1.2 %copy-done = bf16[1,32,128,128]{3,2,1,0:T(8,128)(2,1)S(1)} copy-done((bf16[1,32,128,128]{3,2,1,0:T(8,128)(2,1)S(1)}, bf16[1,32,128,128]{3,2,1,0:T(8,128)(2,1)}, u32[]{:S(2)}) %copy-start) | copy-done | bytes 1048600
  5.4 0.0 copy-start.1
  5.4 0.9 %copy-done.1 = bf16[512,128]{1,0:T(8,128)(2,1)S(1)} copy-done((bf16[512,128]{1,0:T(8,128)(2,1)S(1)}, bf16[512,128]{1,0:T(8,128)(2,1)}, u32[]{:S(2)}) %copy-start.1) | copy-done | bytes 131096
  6.3 53.8 %filter_steps.1 = bf16[512,128]{1,0:T(8,128)(2,1)S(1)} custom-call(bf16[512,128]{1,0:T(8,128)(2,1)S(1)} %copy-done.1, bf16[1,32,128,128]{3,2,1,0:T(8,128)(2,1)S(1)} %copy-done, s32[1,32]{1,0:T(1,128)S(1)} %copy-done.4, s32[1,32]{1,0:T(1,128)S(1)} %copy-done.5, s32[2,32]{1,0:T(2,128)S(1)} %copy-done.2, s32[2,20]{1,0:T(2,128)S(1)} %copy-done.3, ...), custom_call_target="tpu_custom_call" | custom-call | tf_op jit(solution)/shard_map/filter_steps/pallas_call | solution.py:220
  60.1 0.7 %copy.12 = bf16[512,128]{1,0:T(8,128)(2,1)} copy(bf16[512,128]{1,0:T(8,128)(2,1)S(1)} %filter_steps.1) | data formatting | bytes 262144
Async XLA Ops:
  3.5 0.7 %copy-start.3 = (s32[2,20]{1,0:T(2,128)S(1)}, s32[2,20]{1,0:T(2,128)}, u32[]{:S(2)}) copy-start(s32[2,20]{1,0:T(2,128)} %get-tuple-element.8.last_ref) | copy-start | bytes 484
  3.5 0.7 %copy-start.5 = (s32[1,32]{1,0:T(1,128)S(1)}, s32[1,32]{1,0:T(1,128)}, u32[]{:S(2)}) copy-start(s32[1,32]{1,0:T(1,128)} %cols_ref.3) | copy-start | bytes 388
  3.5 0.7 %copy-start.2 = (s32[2,32]{1,0:T(2,128)S(1)}, s32[2,32]{1,0:T(2,128)}, u32[]{:S(2)}) copy-start(s32[2,32]{1,0:T(2,128)} %get-tuple-element.7.prev_ref) | copy-start | bytes 772
  3.5 0.7 %copy-start.4 = (s32[1,32]{1,0:T(1,128)S(1)}, s32[1,32]{1,0:T(1,128)}, u32[]{:S(2)}) copy-start(s32[1,32]{1,0:T(1,128)} %rows_ref.3) | copy-start | bytes 388
  4.2 1.2 %copy-start = (bf16[1,32,128,128]{3,2,1,0:T(8,128)(2,1)S(1)}, bf16[1,32,128,128]{3,2,1,0:T(8,128)(2,1)}, u32[]{:S(2)}) copy-start(bf16[1,32,128,128]{3,2,1,0:T(8,128)(2,1)} %tiles_ref.1) | copy-start | bytes 3145732
  5.4 0.9 %copy-start.1 = (bf16[512,128]{1,0:T(8,128)(2,1)S(1)}, bf16[512,128]{1,0:T(8,128)(2,1)}, u32[]{:S(2)}) copy-start(bf16[512,128]{1,0:T(8,128)(2,1)} %x_ref.1) | copy-start | bytes 393220

commit v2 on v0

v2 whole, which is shorter than its diff:
```python
import functools

import jax
import jax.numpy as jnp
from jax import lax
from jax.experimental import pallas as pl
from jax.experimental.pallas import tpu as pltpu
from jax.sharding import PartitionSpec as P

CHUNKS = 2
UNROLL = 8
MESH_ID = pl.DeviceIdType.MESH
ROW_AT, COL_AT, ROW_PREV, COL_PREV, ROW_LAST, COL_LAST = range(6)


def link_slots(rows_ref, cols_ref, counts_ref, table_ref, *, slots, pt, row_tiles, span):
    e = lax.rem(lax.axis_index("row"), 2)
    for k in range(row_tiles):
        table_ref[ROW_LAST, k] = slots
    for k in range(span):
        table_ref[COL_LAST, k] = slots
    for s in range(slots):
        used = s < counts_ref[0, 0]
        row = rows_ref[0, s]
        col = cols_ref[0, s] + e * pt
        table_ref[ROW_AT, s] = (row // pt * 2 + e) * pt + row % pt
        table_ref[COL_AT, s] = col
        for key, prev, last in ((row, ROW_PREV, ROW_LAST), (col, COL_PREV, COL_LAST)):
            before = table_ref[last, key]
            table_ref[prev, s] = jnp.where(used, before, slots)
            table_ref[last, key] = jnp.where(used, s, before)


def filter_kernel(dims, x_ref, tiles_ref, table_ref, center_ref, width_ref, out_ref, *scratch):
    R, C, hw, pt, slots, vec, size = dims
    vc = vec // 2 // CHUNKS
    unit = 2 * pt
    it = iter(scratch)

    def grid2():
        return [[next(it) for _ in range(CHUNKS)] for _ in range(2)]

    win, seg, row_out, row_in = grid2(), grid2(), grid2(), grid2()
    z_out = [grid2(), grid2()]
    z_in = [grid2(), grid2()]
    back, direct = grid2(), grid2()
    halves, final = next(it), next(it)
    tiles = [next(it), next(it)]
    tabs = [next(it), next(it)]
    tab_land = next(it)
    row_send, row_recv, z_send, z_recv, pair_send, pair_recv, local = (next(it) for _ in range(7))

    r = lax.axis_index("row")
    c = lax.axis_index("col")
    e = lax.rem(r, 2)
    partner = {"row": r + 1 - 2 * e}

    def chip_row(o):
        return {"row": lax.rem(r + 2 * o + R, R)}

    offsets = sorted({2 * o % R for o in range(1, hw + 1)} | {-2 * o % R for o in range(1, hw + 1)})
    barrier = pltpu.get_barrier_semaphore()
    for off in offsets:
        pl.semaphore_signal(barrier, inc=1, device_id={"row": lax.rem(r + off, R)}, device_id_type=MESH_ID)
    for off in (1, C - 1):
        pl.semaphore_signal(barrier, inc=1, device_id={"col": lax.rem(c + off, C)}, device_id_type=MESH_ID)
    pl.semaphore_signal(barrier, inc=1, device_id=partner, device_id_type=MESH_ID)

    own_tiles = pltpu.make_async_copy(tiles_ref.at[0], tiles[0], local.at[0])
    own_table = pltpu.make_async_copy(table_ref, tabs[0], local.at[1])
    own_tiles.start()
    own_table.start()
    for j in range(pt):
        block = x_ref[j * size:(j + 1) * size, :].astype(jnp.float32).T.astype(jnp.bfloat16)
        for a in range(2):
            for h in range(CHUNKS):
                at = (a * CHUNKS + h) * vc
                halves[a, h, j] = block[at:at + vc, :]
    for h in range(CHUNKS):
        for j in range(pt):
            win[0][h][e * pt + j] = halves[e, h, j]
        for side in range(2):
            back[side][h][slots] = jnp.zeros((vc, size), jnp.float32)
            direct[side][h][slots] = jnp.zeros((vc, size), jnp.float32)
    for way, edge in ((0, 0), (1, C - 1)):
        @pl.when(c == edge)
        def _():
            for t in range(2):
                for h in range(CHUNKS):
                    z_in[way][t][h][...] = jnp.zeros((C - 1, unit, vc, size), jnp.bfloat16)
    pl.semaphore_wait(barrier, len(offsets) + 3)

    drains = []

    def remote(src, dst, send, recv, device):
        return pltpu.make_async_remote_copy(
            src_ref=src, dst_ref=dst, send_sem=send, recv_sem=recv,
            device_id=device, device_id_type=MESH_ID)

    def start(copy, valid=None):
        if valid is None:
            copy.start()
        else:
            pl.when(valid)(copy.start)
        drains.append((copy, valid))
        return copy

    def step_wait(copy, valid):
        pl.when(valid)(copy.wait_recv)

    swap = [
        start(remote(halves.at[1 - e, h], win[0][h].at[pl.ds(e * pt, pt)],
                     pair_send.at[h], pair_recv.at[h], partner))
        for h in range(CHUNKS)
    ]
    pair_table = start(remote(table_ref, tab_land, pair_send.at[CHUNKS], pair_recv.at[CHUNKS], partner))
    pair_tiles = start(remote(tiles_ref.at[0], tiles[1], pair_send.at[CHUNKS + 1], pair_recv.at[CHUNKS + 1], partner))

    def has_from(way, d):
        return c - d >= 0 if way == 0 else c + d < C

    def has_to(way, d):
        return has_from(1 - way, d)

    def onward(way):
        return {"col": lax.rem(c + (1 if way == 0 else C - 1), C)}

    def z_gather(t, h, way, d):
        origin = lax.rem(c + (C - d if way == 0 else d), C)
        place = seg[t][h].at[pl.ds(origin * unit, unit)]
        return remote(win[t][h].at[pl.ds(0, unit)] if d == 0 else place, place,
                      z_send.at[t, h, 0, way, d], z_recv.at[t, h, 0, way, d], onward(way))

    def start_gather(t, h):
        for j in range(unit):
            seg[t][h][c * unit + j] = win[t][h][j]
        for way in range(2):
            start(z_gather(t, h, way, 0), has_to(way, 1))
        return [
            start(remote(win[t][h].at[pl.ds(0, unit)], win[t][h].at[pl.ds(o * unit, unit)],
                         row_send.at[t, h, 0, o], row_recv.at[t, h, 0, o], chip_row(-o)))
            for o in range(1, hw + 1)
        ]

    def relay(t, h):
        for d in range(1, C):
            for way in range(2):
                place = lax.rem(c + (C - d if way == 0 else d), C)
                view = seg[t][h].at[pl.ds(place * unit, unit)]
                landed = remote(view, view, z_send.at[t, h, 0, way, d - 1],
                                z_recv.at[t, h, 0, way, d - 1], onward(way))
                step_wait(landed, has_from(way, d))
                if d < C - 1:
                    start(z_gather(t, h, way, d), has_from(way, d) & has_to(way, 1))

    def products(source, side, h, transposed):
        at, prev = (ROW_AT, COL_PREV) if transposed else (COL_AT, ROW_PREV)
        sums = (back if transposed else direct)[side][h]
        contract = (((1,), (0,)), ((), ())) if transposed else (((1,), (1,)), ((), ()))

        def one(s, carry):
            term = lax.dot_general(
                source[tabs[side][at, s]], tiles[side][s], contract,
                preferred_element_type=jnp.float32)
            sums[s] = sums[tabs[side][prev, s]] + term
            return carry

        lax.fori_loop(0, slots, one, 0, unroll=UNROLL)

    def back_sum(h, place):
        return (back[0][h][tabs[0][COL_LAST, place]] + back[1][h][tabs[1][COL_LAST, place]])

    def back_products(t, h):
        for side in range(2):
            products(seg[t][h], side, h, True)
        for o in range(1, hw + 1):
            for m in range(unit):
                row_out[t][h][o - 1, m] = back_sum(h, o * unit + m).astype(jnp.bfloat16)
        return [
            start(remote(row_out[t][h].at[o - 1], row_in[t][h].at[o - 1],
                         row_send.at[t, h, 1, o], row_recv.at[t, h, 1, o], chip_row(o)))
            for o in range(1, hw + 1)
        ]

    def direct_products(t, h, arriving):
        for copy in arriving:
            copy.wait_recv()
        for side in range(2):
            products(win[t][h], side, h, False)

    def landing(t, h, way, d):
        return remote(z_out[way][t][h].at[d], z_in[way][t][h].at[d],
                      z_send.at[t, h, 1, way, d], z_recv.at[t, h, 1, way, d], onward(way))

    def chain(t, h, d):
        for way in range(2):
            step_wait(landing(t, h, way, d), has_from(way, 1) & has_to(way, d)) if d < C - 1 else None

            @pl.when(has_to(way, d))
            def _():
                piece = lax.rem(c + (d if way == 0 else C - d), C)
                for side in range(2):
                    parity = e if side == 0 else 1 - e
                    for j in range(pt):
                        value = direct[side][h][tabs[side][ROW_LAST, piece * pt + j]]
                        if d < C - 1:
                            value += z_in[way][t][h][d, parity * pt + j].astype(jnp.float32)
                        z_out[way][t][h][d - 1, parity * pt + j] = value.astype(jnp.bfloat16)

            start(landing(t, h, way, d - 1), has_to(way, d))

    def combine(t, h, returning):
        for copy in returning:
            copy.wait_recv()
        for way in range(2):
            step_wait(landing(t, h, way, 0), has_from(way, 1))
        shift = center_ref[0]
        width = width_ref[0]
        for side in range(2):
            parity = e if side == 0 else 1 - e
            for j in range(pt):
                m = parity * pt + j
                total = back_sum(h, m) + direct[side][h][tabs[side][ROW_LAST, c * pt + j]]
                for o in range(hw):
                    total += row_in[t][h][o, m].astype(jnp.float32)
                for way in range(2):
                    total += z_in[way][t][h][0, m].astype(jnp.float32)
                begin = win[0][h][m].astype(jnp.float32)
                if t == 0:
                    win[1][h][m] = ((total - shift * begin) / width).astype(jnp.bfloat16)
                else:
                    first = win[1][h][m].astype(jnp.float32)
                    value = (2.0 * (total - shift * first) / width - begin).astype(jnp.bfloat16)
                    if side == 0:
                        final[e, h, j] = value
                    else:
                        halves[e, h, j] = value

    arriving = [None] * CHUNKS
    for h in range(CHUNKS):
        swap[h].wait_recv()
        arriving[h] = start_gather(0, h)
    own_table.wait()
    pair_table.wait_recv()
    other_table = pltpu.make_async_copy(tab_land, tabs[1], local.at[2])
    other_table.start()
    other_table.wait()
    own_tiles.wait()
    pair_tiles.wait_recv()
    for copy in swap:
        copy.wait_send()
        drains.remove((copy, None))
    for t in range(2):
        returning = [None] * CHUNKS
        steps = []
        relay(t, 0)
        for h in range(CHUNKS):
            returning[h] = back_products(t, h)
            if h + 1 < CHUNKS:
                relay(t, h + 1)
            if h:
                for d in range(C - 2, 0, -1):
                    chain(t, h - 1, d)
            direct_products(t, h, arriving[h])
            chain(t, h, C - 1)
        for h in range(CHUNKS):
            if h == CHUNKS - 1:
                for d in range(C - 2, 0, -1):
                    chain(t, h, d)
            combine(t, h, returning[h])
            if t == 0:
                arriving[h] = start_gather(1, h)
            else:
                steps.append(start(remote(
                    halves.at[e, h], final.at[e, h], pair_send.at[CHUNKS + 2 + h],
                    pair_recv.at[CHUNKS + 2 + h], partner)))
    for copy in steps:
        copy.wait_recv()
    for j in range(pt):
        whole = jnp.concatenate(
            [final[a, h, j].astype(jnp.float32) for a in range(2) for h in range(CHUNKS)], axis=0)
        out_ref[j * size:(j + 1) * size, :] = whole.T.astype(jnp.bfloat16)
    for copy, valid in drains:
        if valid is None:
            copy.wait_send()
        else:
            pl.when(valid)(copy.wait_send)


def per_device(start_vectors, tiles, tile_rows, tile_cols, tile_counts, center, half_width):
    R = lax.axis_size("row")
    C = lax.axis_size("col")
    half = R // 2
    hw = half // 2
    piece_rows, vec = start_vectors.shape
    size = tiles.shape[-1]
    slots = tiles.shape[1]
    pt = piece_rows // size
    vc = vec // 2 // CHUNKS
    unit = 2 * pt
    row_tiles = pt * C
    span = pt * (half + 2)
    lanes = pl.cdiv(max(slots, row_tiles, span), 128) * 128
    smem = pl.BlockSpec(memory_space=pltpu.SMEM)
    vmem = pl.BlockSpec(memory_space=pltpu.VMEM)
    anywhere = pl.BlockSpec(memory_space=pl.ANY)
    table = pl.pallas_call(
        functools.partial(link_slots, slots=slots, pt=pt, row_tiles=row_tiles, span=span),
        out_shape=jax.ShapeDtypeStruct((8, lanes), jnp.int32),
        in_specs=[smem] * 3,
        out_specs=smem,
        name="link_slots",
    )(tile_rows, tile_cols, tile_counts)

    bf, f32 = jnp.bfloat16, jnp.float32

    def pair(shape, dtype):
        return [pltpu.VMEM(shape, dtype) for _ in range(2 * CHUNKS)]

    scratch = (
        pair(((hw + 1) * unit, vc, size), bf)
        + pair((C * unit, vc, size), bf)
        + pair((hw, unit, vc, size), bf)
        + pair((hw, unit, vc, size), bf)
        + pair((C - 1, unit, vc, size), bf) * 2
        + pair((C - 1, unit, vc, size), bf) * 2
        + pair((slots + 1, vc, size), f32) * 2
        + [pltpu.VMEM((2, CHUNKS, pt, vc, size), bf)] * 2
        + [pltpu.VMEM((slots, size, size), bf)] * 2
        + [pltpu.SMEM((8, lanes), jnp.int32)] * 2
        + [pltpu.VMEM((8, lanes), jnp.int32)]
        + [pltpu.SemaphoreType.DMA((2, CHUNKS, 2, hw + 1))] * 2
        + [pltpu.SemaphoreType.DMA((2, CHUNKS, 2, 2, C))] * 2
        + [pltpu.SemaphoreType.DMA((2 * CHUNKS + 2,))] * 2
        + [pltpu.SemaphoreType.DMA((3,))]
    )
    return pl.pallas_call(
        functools.partial(filter_kernel, (R, C, hw, pt, slots, vec, size)),
        out_shape=jax.ShapeDtypeStruct((piece_rows, vec), bf),
        in_specs=[vmem, anywhere, anywhere, smem, smem],
        out_specs=vmem,
        scratch_shapes=scratch,
        compiler_params=pltpu.CompilerParams(
            collective_id=0, has_side_effects=True, vmem_limit_bytes=40 << 20),
        name="filter_steps",
    )(start_vectors, tiles, table, center, half_width)


def solution(mesh):
    return jax.shard_map(
        per_device,
        mesh=mesh,
        in_specs=(
            P(("row", "col"), None),
            P("row", "col", None, None),
            P("row", "col"),
            P("row", "col"),
            P("row", "col"),
            P(),
            P(),
        ),
        out_specs=P(("row", "col"), None),
        check_vma=False,
    )
```

time: 148 us -> 83.2 us (0.56)
  Pallas kernels: 0 us -> 77.5 us
  blocking collectives: 41.6 us -> 0 us
  waiting for transfers between devices: 41.4 us -> 0 us
  matrix products: 14.7 us -> 0 us
  local copies, waits for them, and re-layouts: 17.4 us -> 3.47 us
  between operations: 15.7 us -> 1.97 us
  starting transfers between devices: 10.9 us -> 0 us
  other arithmetic: 5.56 us -> 0 us
    pallas_call x0 -> x2, Pallas kernels: none -> 77.5 us  [the longest x1 75.7 us: per_device(): pl.pallas_call(functools.partial(filter_kernel, (R, C, hw, pt, slots, vec...]
    all_gather x2 -> x0, blocking collectives: 41.6 us -> none  [gather_vectors(): return lax.all_gather(vector_piece, 'col', axis=0, tiled=True)]
    ppermute x12 -> x0, waiting for transfers between devices: 41.4 us -> none  [passed_along(): return lax.ppermute(x, axis, [(i, (i + by) % peers) for i in range(peers)])]
    dot_general x8 -> x0, matrix products: 14.7 us -> none  [the longest x2 4.78 us: direct_rows(): jnp.einsum('it,tan->ian', row_select, products, precision=lax.Precision.H...]
    dot_general x6 -> x0, local copies, waits for them, and re-layouts: 11.5 us -> none  [the longest x2 4.77 us: transposed_piece(): jnp.einsum('tab,tan->tbn', my_tiles, inputs, preferred_element_type=jnp.f...]
    ppermute x12 -> x0, starting transfers between devices: 10.8 us -> none  [passed_along(): return lax.ppermute(x, axis, [(i, (i + by) % peers) for i in range(peers)])]
    gather x4 -> x0, local copies, waits for them, and re-layouts: 4.82 us -> none  [the longest x2 3.32 us: direct_terms(): window.reshape(blocks * piece_tiles, tile_size, vec_count)[cols_list]]
    unnamed x8 -> x7, local copies, waits for them, and re-layouts: 0.02 us -> 3.47 us
  transfers between devices with their start and end apart: 14 -> 0, of which waited for: 10 -> 0; matrix products, arithmetic and copies ran while one was open for 10% -> 0% of each run, Pallas kernels for 0% -> 0%
where the time goes in v2:
time: 83.2 us; the launch traced here: 82.9 us
  Pallas kernels  77.5 us (93%)
  local copies, waits for them, and re-layouts  3.47 us (4%)
  between operations  1.97 us (2%)
    pallas_call x1, Pallas kernels, per_device(): pl.pallas_call(functools.partial(filter_kernel, (R, C, hw, pt, slots, vec...  75.7 us
    unnamed x7, local copies, waits for them, and re-layouts  3.47 us
    pallas_call x1, Pallas kernels, per_device(): pl.pallas_call(functools.partial(link_slots, slots=slots, pt=pt, row_tile...  1.78 us

profile of v2, /device:TPU:0, one launch (start us, length us, event | category | flops | bytes accessed | tf_op | source)
XLA Modules:
  0.0 82.9 jit_solution(11983924748872843513)
XLA Ops:
  1.9 1.8 %link_slots.1.table_ref = s32[8,128]{1,0:T(8,128)} custom-call(s32[1,32]{1,0:T(1,128)} %rows_ref.1, s32[1,32]{1,0:T(1,128)} %cols_ref.1, s32[1,1]{1,0:T(1,128)S(6)} %copy.9.counts_ref), custom_call_target="tpu_custom_call" | custom-call | tf_op jit(solution)/shard_map/link_slots/pallas_call | solution.py:307
  3.7 0.0 copy-start
  3.7 1.2 %copy-done = bf16[1,32,128,128]{3,2,1,0:T(8,128)(2,1)S(1)} copy-done((bf16[1,32,128,128]{3,2,1,0:T(8,128)(2,1)S(1)}, bf16[1,32,128,128]{3,2,1,0:T(8,128)(2,1)}, u32[]{:S(2)}) %copy-start) | copy-done | bytes 1048600
  5.0 0.0 copy-start.1
  5.0 0.9 %copy-done.1 = bf16[512,128]{1,0:T(8,128)(2,1)S(1)} copy-done((bf16[512,128]{1,0:T(8,128)(2,1)S(1)}, bf16[512,128]{1,0:T(8,128)(2,1)}, u32[]{:S(2)}) %copy-start.1) | copy-done | bytes 131096
  5.9 0.0 copy-start.2
  5.9 0.7 copy-done.2
  6.5 75.7 %filter_steps.1 = bf16[512,128]{1,0:T(8,128)(2,1)S(1)} custom-call(bf16[512,128]{1,0:T(8,128)(2,1)S(1)} %copy-done.1, bf16[1,32,128,128]{3,2,1,0:T(8,128)(2,1)S(1)} %copy-done, s32[8,128]{1,0:T(8,128)S(1)} %copy-done.2, f32[1]{0:T(128)S(6)} %copy.10.center_ref, f32[1]{0:T(128)S(6)} %copy.11.width_ref), custom_call_target="tpu_custom_call" | custom-call | tf_op jit(solution)/shard_map/filter_steps/pallas_call | solution.py:337
  82.3 0.7 copy.12
Async XLA Ops:
  3.7 1.2 %copy-start = (bf16[1,32,128,128]{3,2,1,0:T(8,128)(2,1)S(1)}, bf16[1,32,128,128]{3,2,1,0:T(8,128)(2,1)}, u32[]{:S(2)}) copy-start(bf16[1,32,128,128]{3,2,1,0:T(8,128)(2,1)} %tiles_ref.1) | copy-start | bytes 3145732
  5.0 0.9 %copy-start.1 = (bf16[512,128]{1,0:T(8,128)(2,1)S(1)}, bf16[512,128]{1,0:T(8,128)(2,1)}, u32[]{:S(2)}) copy-start(bf16[512,128]{1,0:T(8,128)(2,1)} %x_ref.1) | copy-start | bytes 393220
  5.9 0.7 copy-start.2

commit v3 on v2

--- a/solution.py
+++ b/solution.py
@@ -41,8 +41,7 @@
         return [[next(it) for _ in range(CHUNKS)] for _ in range(2)]
 
     win, seg, row_out, row_in = grid2(), grid2(), grid2(), grid2()
-    z_out = [grid2(), grid2()]
-    z_in = [grid2(), grid2()]
+    z_out, z_in, z_mid = grid2(), grid2(), grid2()
     back, direct = grid2(), grid2()
     halves, final = next(it), next(it)
     tiles = [next(it), next(it)]
@@ -62,7 +61,7 @@
     barrier = pltpu.get_barrier_semaphore()
     for off in offsets:
         pl.semaphore_signal(barrier, inc=1, device_id={"row": lax.rem(r + off, R)}, device_id_type=MESH_ID)
-    for off in (1, C - 1):
+    for off in range(1, C):
         pl.semaphore_signal(barrier, inc=1, device_id={"col": lax.rem(c + off, C)}, device_id_type=MESH_ID)
     pl.semaphore_signal(barrier, inc=1, device_id=partner, device_id_type=MESH_ID)
 
@@ -82,13 +81,30 @@
         for side in range(2):
             back[side][h][slots] = jnp.zeros((vc, size), jnp.float32)
             direct[side][h][slots] = jnp.zeros((vc, size), jnp.float32)
-    for way, edge in ((0, 0), (1, C - 1)):
-        @pl.when(c == edge)
+    first_end, last_end = c == 0, c == C - 1
+    inner = jnp.logical_not(first_end | last_end)
+
+    def gives_to(d):
+        to = lax.rem(c + d, C)
+        to_inner = (to > 0) & (to < C - 1)
+        return to_inner | ((to == 0) & (c == 1)) | ((to == C - 1) & (c == C - 2))
+
+    def takes_from(d):
+        source = lax.rem(c + d, C)
+        return (((source > 0) & (source < C - 1)) | ((source == 0) & (c == 1))
+                | ((source == C - 1) & (c == C - 2)))
+
+    def helps(end, d):
+        other = lax.rem(c + d, C)
+        return (c == 1) & (other >= 2) if end == 0 else (c == C - 2) & (other <= C - 3)
+
+    for d in range(1, C):
+        @pl.when(jnp.logical_not(takes_from(d)))
         def _():
             for t in range(2):
                 for h in range(CHUNKS):
-                    z_in[way][t][h][...] = jnp.zeros((C - 1, unit, vc, size), jnp.bfloat16)
-    pl.semaphore_wait(barrier, len(offsets) + 3)
+                    z_in[t][h][d - 1] = jnp.zeros((unit, vc, size), jnp.bfloat16)
+    pl.semaphore_wait(barrier, len(offsets) + C)
 
     drains = []
 
@@ -116,26 +132,27 @@
     pair_table = start(remote(table_ref, tab_land, pair_send.at[CHUNKS], pair_recv.at[CHUNKS], partner))
     pair_tiles = start(remote(tiles_ref.at[0], tiles[1], pair_send.at[CHUNKS + 1], pair_recv.at[CHUNKS + 1], partner))
 
-    def has_from(way, d):
-        return c - d >= 0 if way == 0 else c + d < C
-
-    def has_to(way, d):
-        return has_from(1 - way, d)
-
-    def onward(way):
-        return {"col": lax.rem(c + (1 if way == 0 else C - 1), C)}
-
-    def z_gather(t, h, way, d):
-        origin = lax.rem(c + (C - d if way == 0 else d), C)
-        place = seg[t][h].at[pl.ds(origin * unit, unit)]
-        return remote(win[t][h].at[pl.ds(0, unit)] if d == 0 else place, place,
-                      z_send.at[t, h, 0, way, d], z_recv.at[t, h, 0, way, d], onward(way))
+    near_first = sorted(range(1, C), key=lambda d: min(d, C - d))
+
+    def z_unit(t, h, origin):
+        return seg[t][h].at[pl.ds(origin * unit, unit)]
+
+    def z_gather(t, h, d):
+        return remote(win[t][h].at[pl.ds(0, unit)], z_unit(t, h, c),
+                      z_send.at[t, h, 0, d], z_recv.at[t, h, 0, C - d],
+                      {"col": lax.rem(c + d, C)})
+
+    def z_forward(t, h, end, d):
+        view = z_unit(t, h, lax.rem(c + d, C))
+        slot = (1 + d) % C if end == 0 else d - 1
+        return remote(view, view, z_send.at[t, h, 1 + end, d], z_recv.at[t, h, 0, slot],
+                      {"col": lax.rem(c + (C - 1 if end == 0 else 1), C)})
 
     def start_gather(t, h):
         for j in range(unit):
             seg[t][h][c * unit + j] = win[t][h][j]
-        for way in range(2):
-            start(z_gather(t, h, way, 0), has_to(way, 1))
+        for d in reversed(near_first):
+            start(z_gather(t, h, d), gives_to(d))
         return [
             start(remote(win[t][h].at[pl.ds(0, unit)], win[t][h].at[pl.ds(o * unit, unit)],
                          row_send.at[t, h, 0, o], row_recv.at[t, h, 0, o], chip_row(-o)))
@@ -143,15 +160,13 @@
         ]
 
     def relay(t, h):
-        for d in range(1, C):
-            for way in range(2):
-                place = lax.rem(c + (C - d if way == 0 else d), C)
-                view = seg[t][h].at[pl.ds(place * unit, unit)]
-                landed = remote(view, view, z_send.at[t, h, 0, way, d - 1],
-                                z_recv.at[t, h, 0, way, d - 1], onward(way))
-                step_wait(landed, has_from(way, d))
-                if d < C - 1:
-                    start(z_gather(t, h, way, d), has_from(way, d) & has_to(way, 1))
+        for d in near_first:
+            view = z_unit(t, h, lax.rem(c + d, C))
+            remote(view, view, z_send.at[t, h, 0, d], z_recv.at[t, h, 0, d],
+                   {"col": lax.rem(c + d, C)}).wait_recv()
+            for end in range(2):
+                if (1 + d if end == 0 else d - 1) % C:
+                    start(z_forward(t, h, end, d), helps(end, d))
 
     def products(source, side, h, transposed):
         at, prev = (ROW_AT, COL_PREV) if transposed else (COL_AT, ROW_PREV)
@@ -188,32 +203,64 @@
         for side in range(2):
             products(win[t][h], side, h, False)
 
-    def landing(t, h, way, d):
-        return remote(z_out[way][t][h].at[d], z_in[way][t][h].at[d],
-                      z_send.at[t, h, 1, way, d], z_recv.at[t, h, 1, way, d], onward(way))
-
-    def chain(t, h, d):
-        for way in range(2):
-            step_wait(landing(t, h, way, d), has_from(way, 1) & has_to(way, d)) if d < C - 1 else None
-
-            @pl.when(has_to(way, d))
+    def z_sums(t, h, d, end=None):
+        piece = lax.rem(c + d, C)
+        for side in range(2):
+            parity = e if side == 0 else 1 - e
+            for j in range(pt):
+                value = direct[side][h][tabs[side][ROW_LAST, piece * pt + j]]
+                if end is not None:
+                    value += z_mid[t][h][d - 1, parity * pt + j].astype(jnp.float32)
+                z_out[t][h][d - 1, parity * pt + j] = value.astype(jnp.bfloat16)
+
+    def z_return(t, h, d):
+        return remote(z_out[t][h].at[d - 1], z_in[t][h].at[C - d - 1],
+                      z_send.at[t, h, 3, d], z_recv.at[t, h, 1, C - d],
+                      {"col": lax.rem(c + d, C)})
+
+    def z_to_mid(t, h, end, d):
+        slot = d - 1 if end == 0 else (d + 1) % C
+        return remote(z_out[t][h].at[d - 1], z_mid[t][h].at[slot - 1],
+                      z_send.at[t, h, 4 + end, d], z_recv.at[t, h, 2, slot],
+                      {"col": lax.rem(c + (1 if end == 0 else C - 1), C)})
+
+    def return_plain(t, h):
+        for d in reversed(near_first):
+            plain = jnp.logical_not(helps(0, d) | helps(1, d))
+
+            @pl.when(plain)
             def _():
-                piece = lax.rem(c + (d if way == 0 else C - d), C)
-                for side in range(2):
-                    parity = e if side == 0 else 1 - e
-                    for j in range(pt):
-                        value = direct[side][h][tabs[side][ROW_LAST, piece * pt + j]]
-                        if d < C - 1:
-                            value += z_in[way][t][h][d, parity * pt + j].astype(jnp.float32)
-                        z_out[way][t][h][d - 1, parity * pt + j] = value.astype(jnp.bfloat16)
-
-            start(landing(t, h, way, d - 1), has_to(way, d))
+                z_sums(t, h, d)
+
+            straight = inner
+            if d == 1:
+                straight = straight | first_end
+            if d == C - 1:
+                straight = straight | last_end
+            start(z_return(t, h, d), straight & plain)
+            if d >= 2:
+                start(z_to_mid(t, h, 0, d), first_end)
+            if d <= C - 2:
+                start(z_to_mid(t, h, 1, d), last_end)
+
+    def return_helped(t, h):
+        for d in reversed(near_first):
+            helped = helps(0, d) | helps(1, d)
+
+            @pl.when(helped)
+            def _():
+                remote(z_out[t][h].at[d - 1], z_mid[t][h].at[d - 1], z_send.at[t, h, 3, d],
+                       z_recv.at[t, h, 2, d], {"col": lax.rem(c + d, C)}).wait_recv()
+                z_sums(t, h, d, 0)
+
+            start(z_return(t, h, d), helped)
 
     def combine(t, h, returning):
         for copy in returning:
             copy.wait_recv()
-        for way in range(2):
-            step_wait(landing(t, h, way, 0), has_from(way, 1))
+        for d in range(1, C):
+            step_wait(remote(z_out[t][h].at[d - 1], z_in[t][h].at[d - 1], z_send.at[t, h, 3, d],
+                             z_recv.at[t, h, 1, d], {"col": lax.rem(c + d, C)}), takes_from(d))
         shift = center_ref[0]
         width = width_ref[0]
         for side in range(2):
@@ -223,8 +270,8 @@
                 total = back_sum(h, m) + direct[side][h][tabs[side][ROW_LAST, c * pt + j]]
                 for o in range(hw):
                     total += row_in[t][h][o, m].astype(jnp.float32)
-                for way in range(2):
-                    total += z_in[way][t][h][0, m].astype(jnp.float32)
+                for d in range(C - 1):
+                    total += z_in[t][h][d, m].astype(jnp.float32)
                 begin = win[0][h][m].astype(jnp.float32)
                 if t == 0:
                     win[1][h][m] = ((total - shift * begin) / width).astype(jnp.bfloat16)
@@ -259,14 +306,11 @@
             if h + 1 < CHUNKS:
                 relay(t, h + 1)
             if h:
-                for d in range(C - 2, 0, -1):
-                    chain(t, h - 1, d)
+                return_helped(t, h - 1)
             direct_products(t, h, arriving[h])
-            chain(t, h, C - 1)
+            return_plain(t, h)
+        return_helped(t, CHUNKS - 1)
         for h in range(CHUNKS):
-            if h == CHUNKS - 1:
-                for d in range(C - 2, 0, -1):
-                    chain(t, h, d)
             combine(t, h, returning[h])
             if t == 0:
                 arriving[h] = start_gather(1, h)
@@ -322,15 +366,14 @@
         + pair((C * unit, vc, size), bf)
         + pair((hw, unit, vc, size), bf)
         + pair((hw, unit, vc, size), bf)
-        + pair((C - 1, unit, vc, size), bf) * 2
-        + pair((C - 1, unit, vc, size), bf) * 2
+        + pair((C - 1, unit, vc, size), bf) * 3
         + pair((slots + 1, vc, size), f32) * 2
         + [pltpu.VMEM((2, CHUNKS, pt, vc, size), bf)] * 2
         + [pltpu.VMEM((slots, size, size), bf)] * 2
         + [pltpu.SMEM((8, lanes), jnp.int32)] * 2
         + [pltpu.VMEM((8, lanes), jnp.int32)]
         + [pltpu.SemaphoreType.DMA((2, CHUNKS, 2, hw + 1))] * 2
-        + [pltpu.SemaphoreType.DMA((2, CHUNKS, 2, 2, C))] * 2
+        + [pltpu.SemaphoreType.DMA((2, CHUNKS, 6, C))] * 2
         + [pltpu.SemaphoreType.DMA((2 * CHUNKS + 2,))] * 2
         + [pltpu.SemaphoreType.DMA((3,))]
     )

time: 83.2 us -> 71.2 us (0.86)
  Pallas kernels: 77.5 us -> 65.4 us
    pallas_call x1, Pallas kernels: 75.7 us -> 63.7 us  [per_device(): pl.pallas_call(functools.partial(filter_kernel, (R, C, hw, pt, slots, vec...]
where the time goes in v3:
time: 71.2 us; the launch traced here: 70.9 us
  Pallas kernels  65.4 us (92%)
  local copies, waits for them, and re-layouts  3.47 us (5%)
  between operations  1.97 us (3%)
    pallas_call x1, Pallas kernels, per_device(): pl.pallas_call(functools.partial(filter_kernel, (R, C, hw, pt, slots, vec...  63.7 us
    unnamed x7, local copies, waits for them, and re-layouts  3.47 us
    pallas_call x1, Pallas kernels, per_device(): pl.pallas_call(functools.partial(link_slots, slots=slots, pt=pt, row_tile...  1.78 us

profile of v3, /device:TPU:0, one launch (start us, length us, event | category | flops | bytes accessed | tf_op | source)
XLA Modules:
  0.0 70.9 jit_solution(2976639812720608187)
XLA Ops:
  1.9 1.8 %link_slots.1.table_ref = s32[8,128]{1,0:T(8,128)} custom-call(s32[1,32]{1,0:T(1,128)} %rows_ref.1, s32[1,32]{1,0:T(1,128)} %cols_ref.1, s32[1,1]{1,0:T(1,128)S(6)} %copy.9.counts_ref), custom_call_target="tpu_custom_call" | custom-call | tf_op jit(solution)/shard_map/link_slots/pallas_call | solution.py:351
  3.7 0.0 copy-start
  3.7 1.2 %copy-done = bf16[1,32,128,128]{3,2,1,0:T(8,128)(2,1)S(1)} copy-done((bf16[1,32,128,128]{3,2,1,0:T(8,128)(2,1)S(1)}, bf16[1,32,128,128]{3,2,1,0:T(8,128)(2,1)}, u32[]{:S(2)}) %copy-start) | copy-done | bytes 1048600
  5.0 0.0 copy-start.1
  5.0 0.9 %copy-done.1 = bf16[512,128]{1,0:T(8,128)(2,1)S(1)} copy-done((bf16[512,128]{1,0:T(8,128)(2,1)S(1)}, bf16[512,128]{1,0:T(8,128)(2,1)}, u32[]{:S(2)}) %copy-start.1) | copy-done | bytes 131096
  5.9 0.0 copy-start.2
  5.9 0.7 copy-done.2
  6.5 63.7 %filter_steps.1 = bf16[512,128]{1,0:T(8,128)(2,1)S(1)} custom-call(bf16[512,128]{1,0:T(8,128)(2,1)S(1)} %copy-done.1, bf16[1,32,128,128]{3,2,1,0:T(8,128)(2,1)S(1)} %copy-done, s32[8,128]{1,0:T(8,128)S(1)} %copy-done.2, f32[1]{0:T(128)S(6)} %copy.10.center_ref, f32[1]{0:T(128)S(6)} %copy.11.width_ref), custom_call_target="tpu_custom_call" | custom-call | tf_op jit(solution)/shard_map/filter_steps/pallas_call | solution.py:380
  70.2 0.7 copy.12
Async XLA Ops:
  3.7 1.2 %copy-start = (bf16[1,32,128,128]{3,2,1,0:T(8,128)(2,1)S(1)}, bf16[1,32,128,128]{3,2,1,0:T(8,128)(2,1)}, u32[]{:S(2)}) copy-start(bf16[1,32,128,128]{3,2,1,0:T(8,128)(2,1)} %tiles_ref.1) | copy-start | bytes 3145732
  5.0 0.9 %copy-start.1 = (bf16[512,128]{1,0:T(8,128)(2,1)S(1)}, bf16[512,128]{1,0:T(8,128)(2,1)}, u32[]{:S(2)}) copy-start(bf16[512,128]{1,0:T(8,128)(2,1)} %x_ref.1) | copy-start | bytes 393220
  5.9 0.7 copy-start.2

commit v4 on v1

--- a/solution.py
+++ b/solution.py
@@ -39,7 +39,9 @@
     col_in = [[next(it) for _ in range(CHUNKS)] for _ in range(2)]
     back = [next(it) for _ in range(CHUNKS)]
     direct = [next(it) for _ in range(CHUNKS)]
+    mid = [[next(it) for _ in range(CHUNKS)] for _ in range(2)]
     result = next(it)
+    tiles, local = next(it), next(it)
     row_send, row_recv, col_send, col_recv = (next(it) for _ in range(4))
 
     r = lax.axis_index("row")
@@ -52,6 +54,14 @@
     for off in range(1, C):
         pl.semaphore_signal(barrier, inc=1, device_id={"col": lax.rem(c + off, C)}, device_id_type=MESH_ID)
 
+    fetch = pltpu.make_async_copy(tiles_ref.at[0], tiles, local)
+    fetch.start()
+    for end, slot in ((0, 0), (C - 1, C - 2)):
+        @pl.when(c == end)
+        def _():
+            for t in range(2):
+                for h in range(CHUNKS):
+                    col_in[t][h][slot] = jnp.zeros((pt, vc, size), jnp.bfloat16)
     for j in range(pt):
         block = x_ref[j * size:(j + 1) * size, :].astype(jnp.float32).T.astype(jnp.bfloat16)
         for h in range(CHUNKS):
@@ -101,6 +111,84 @@
 
     started = []
 
+    def not_far(d):
+        if d == C - 1:
+            return c != 0
+        return c != C - 1 if d == 1 else None
+
+    def near_far(d):
+        cond = None
+        if d == 2:
+            cond = c == C - 2
+        if d == C - 2:
+            cond = c == 1 if cond is None else cond | (c == 1)
+        return cond
+
+    def when(cond, act):
+        if cond is None:
+            act()
+        else:
+            pl.when(cond)(act)
+
+    def start_if(copy, cond):
+        when(cond, copy.start)
+        drains.append((copy, cond))
+
+    drains = []
+
+    def forward(t, h, end):
+        view = seg[t][h].at[pl.ds(end * pt, pt)]
+        slot = 1 if end else C - 1
+        return pltpu.make_async_remote_copy(
+            src_ref=view, dst_ref=view,
+            send_sem=col_send.at[t, h, 2, 0], recv_sem=col_recv.at[t, h, 0, slot],
+            device_id={"col": lax.rem(c + (C - 1 if end else 1), C)}, device_id_type=MESH_ID)
+
+    def to_mid(t, h, d):
+        return pltpu.make_async_remote_copy(
+            src_ref=col_out[t][h].at[d - 1], dst_ref=mid[t][h],
+            send_sem=col_send.at[t, h, 1, d], recv_sem=col_recv.at[t, h, 1, 0],
+            device_id={"col": lax.rem(c + C - d, C)}, device_id_type=MESH_ID)
+
+    def start_gather(t, h):
+        cols, rows = gather_copies(t, h)
+        for d in sorted(range(1, C), key=lambda d: -min(d, C - d)):
+            start_if(cols[d - 1], not_far(d))
+        return cols, start_all(rows)
+
+    def col_sums(t, h, d, helped):
+        piece = lax.rem(c + d, C)
+        for j in range(pt):
+            value = direct[h][last_ref[0, piece * pt + j]]
+            if helped:
+                value += mid[t][h][j].astype(jnp.float32)
+            col_out[t][h][d - 1, j] = value.astype(jnp.bfloat16)
+
+    def return_plain(t, h):
+        copies = col_returns(t, h)
+        for d in sorted(range(1, C), key=lambda d: min(d, C - d)):
+            helped = near_far(d)
+            plain = None if helped is None else jnp.logical_not(helped)
+            when(plain, lambda: col_sums(t, h, d, False))
+            straight = not_far(d)
+            if straight is not None:
+                start_if(to_mid(t, h, d), jnp.logical_not(straight))
+            both = straight if plain is None else plain if straight is None else plain & straight
+            start_if(copies[d - 1], both)
+        return copies
+
+    def return_helped(t, h):
+        copies = col_returns(t, h)
+        for d in range(1, C):
+            helped = near_far(d)
+            if helped is not None:
+                def add():
+                    to_mid(t, h, d).wait_recv()
+                    col_sums(t, h, d, True)
+
+                when(helped, add)
+                start_if(copies[d - 1], helped)
+
     def start_all(copies):
         for copy in copies:
             copy.start()
@@ -112,7 +200,7 @@
 
         def one(s, carry):
             term = lax.dot_general(
-                source[index_ref[0, s]], tiles_ref[0, s], contract,
+                source[index_ref[0, s]], tiles[s], contract,
                 preferred_element_type=jnp.float32)
             sums[s] = sums[prev_ref[side, s]] + term
             return carry
@@ -121,21 +209,25 @@
 
     def compute(t, h, copies):
         cols, rows = copies
-        for copy in cols:
-            copy.wait_recv()
+        for d in sorted(range(1, C), key=lambda d: -min(d, C - d)):
+            cols[d - 1].wait_recv()
+            if d == C - 2:
+                start_if(forward(t, h, 0), c == C - 2)
+            if d == 2:
+                start_if(forward(t, h, C - 1), c == 1)
+        if t == 0 and h == 0:
+            fetch.wait()
         products(seg[t][h], rows_ref, 1, back[h], True)
         for b in range(1, half + 1):
             for j in range(pt):
                 row_out[t][h][b - 1, j] = back[h][last_ref[1, b * pt + j]].astype(jnp.bfloat16)
         returns = start_all(row_returns(t, h))
+        if h:
+            return_helped(t, h - 1)
         for copy in rows:
             copy.wait_recv()
         products(win[t][h], cols_ref, 0, direct[h], False)
-        for d in range(1, C):
-            piece = lax.rem(c + d, C)
-            for j in range(pt):
-                col_out[t][h][d - 1, j] = direct[h][last_ref[0, piece * pt + j]].astype(jnp.bfloat16)
-        return returns, start_all(col_returns(t, h))
+        return returns, return_plain(t, h)
 
     def applied(t, h, returns, j):
         total = back[h][last_ref[1, j]] + direct[h][last_ref[0, c * pt + j]]
@@ -149,14 +241,16 @@
     width = width_ref[0]
     gathers = [None] * CHUNKS
     for h in range(CHUNKS):
-        cols, rows = gather_copies(0, h)
-        gathers[h] = (start_all(cols), start_all(rows))
+        gathers[h] = start_gather(0, h)
     for t in range(2):
         returns = [compute(t, h, gathers[h]) for h in range(CHUNKS)]
+        return_helped(t, CHUNKS - 1)
         for h in range(CHUNKS):
-            for group in returns[h]:
-                for copy in group:
-                    copy.wait_recv()
+            for copy in returns[h][0]:
+                copy.wait_recv()
+            for d in range(1, C):
+                taken = c != 0 if d == 1 else c != C - 1 if d == C - 1 else None
+                when(taken, returns[h][1][d - 1].wait_recv)
             for j in range(pt):
                 begin = win[0][h][j].astype(jnp.float32)
                 if t == 0:
@@ -168,12 +262,13 @@
                     value = 2.0 * (applied(t, h, returns, j) - shift * first) / width - begin
                     result[j, h * vc:(h + 1) * vc, :] = value
             if t == 0:
-                cols, rows = gather_copies(1, h)
-                gathers[h] = (start_all(cols), start_all(rows))
+                gathers[h] = start_gather(1, h)
     for j in range(pt):
         out_ref[j * size:(j + 1) * size, :] = result[j].T.astype(jnp.bfloat16)
     for copy in started:
         copy.wait_send()
+    for copy, cond in drains:
+        when(cond, copy.wait_send)
 
 
 def per_device(start_vectors, tiles, tile_rows, tile_cols, tile_counts, center, half_width):
@@ -213,14 +308,15 @@
         + pair((half, pt, vc, size), bf)
         + pair((C - 1, pt, vc, size), bf)
         + [pltpu.VMEM((slots + 1, vc, size), f32) for _ in range(2 * CHUNKS)]
-        + [pltpu.VMEM((pt, vec, size), f32)]
+        + pair((pt, vc, size), bf)
+        + [pltpu.VMEM((pt, vec, size), f32), pltpu.VMEM((slots, size, size), bf), pltpu.SemaphoreType.DMA]
         + [pltpu.SemaphoreType.DMA((2, CHUNKS, 2, half + 1))] * 2
-        + [pltpu.SemaphoreType.DMA((2, CHUNKS, 2, C))] * 2
+        + [pltpu.SemaphoreType.DMA((2, CHUNKS, 3, C))] * 2
     )
     return pl.pallas_call(
         functools.partial(filter_kernel, (R, C, half, pt, slots, vec, size)),
         out_shape=jax.ShapeDtypeStruct((piece_rows, vec), bf),
-        in_specs=[vmem, vmem, smem, smem, smem, smem, smem, smem],
+        in_specs=[vmem, pl.BlockSpec(memory_space=pl.ANY), smem, smem, smem, smem, smem, smem],
         out_specs=vmem,
         scratch_shapes=scratch,
         compiler_params=pltpu.CompilerParams(

time: 61 us -> 58.3 us (0.956)
  Pallas kernels: 55.3 us -> 52.6 us
    pallas_call x1, Pallas kernels: 53.8 us -> 51 us  [per_device(): pl.pallas_call(functools.partial(filter_kernel, (R, C, half, pt, slots, v...]
where the time goes in v4:
time: 58.3 us; the launch traced here: 58 us
  Pallas kernels  52.6 us (90%)
  local copies, waits for them, and re-layouts  3.46 us (6%)
  between operations  1.99 us (3%)
    pallas_call x1, Pallas kernels, per_device(): pl.pallas_call(functools.partial(filter_kernel, (R, C, half, pt, slots, v...  51 us
    unnamed x13, local copies, waits for them, and re-layouts  3.46 us
    pallas_call x1, Pallas kernels, per_device(): pl.pallas_call(functools.partial(link_slots, slots=slots, row_tiles=row_t...  1.56 us

profile of v4, /device:TPU:0, one launch (start us, length us, event | category | flops | bytes accessed | tf_op | source)
XLA Modules:
  0.0 58.0 jit_solution(17055824174615546358)
XLA Ops:
  1.9 1.6 %link_slots.1 = (s32[2,32]{1,0:T(2,128)}, s32[2,20]{1,0:T(2,128)}) custom-call(s32[1,32]{1,0:T(1,128)} %rows_ref.3, s32[1,32]{1,0:T(1,128)} %cols_ref.3, s32[1,1]{1,0:T(1,128)S(6)} %copy.9.counts_ref), custom_call_target="tpu_custom_call" | custom-call | tf_op jit(solution)/shard_map/link_slots/pallas_call | solution.py:287
  3.5 0.0 copy-start.3
  3.5 0.0 copy-start.5
  3.5 0.0 copy-start.2
  3.5 0.0 copy-start.4
  3.6 0.6 %copy-done.3 = s32[2,20]{1,0:T(2,128)S(1)} copy-done((s32[2,20]{1,0:T(2,128)S(1)}, s32[2,20]{1,0:T(2,128)}, u32[]{:S(2)}) %copy-start.3) | copy-done | bytes 184
  4.2 0.0 copy-done.5
  4.2 0.0 copy-done.2
  4.2 0.0 copy-done.4
  4.2 0.0 copy-start
  4.2 1.2 %copy-done = bf16[1,32,128,128]{3,2,1,0:T(8,128)(2,1)S(1)} copy-done((bf16[1,32,128,128]{3,2,1,0:T(8,128)(2,1)S(1)}, bf16[1,32,128,128]{3,2,1,0:T(8,128)(2,1)}, u32[]{:S(2)}) %copy-start) | copy-done | bytes 1048600
  5.4 0.0 copy-start.1
  5.5 0.9 %copy-done.1 = bf16[512,128]{1,0:T(8,128)(2,1)S(1)} copy-done((bf16[512,128]{1,0:T(8,128)(2,1)S(1)}, bf16[512,128]{1,0:T(8,128)(2,1)}, u32[]{:S(2)}) %copy-start.1) | copy-done | bytes 131096
  6.4 51.0 %filter_steps.1 = bf16[512,128]{1,0:T(8,128)(2,1)S(1)} custom-call(bf16[512,128]{1,0:T(8,128)(2,1)S(1)} %copy-done.1, bf16[1,32,128,128]{3,2,1,0:T(8,128)(2,1)S(1)} %copy-done, s32[1,32]{1,0:T(1,128)S(1)} %copy-done.4, s32[1,32]{1,0:T(1,128)S(1)} %copy-done.5, s32[2,32]{1,0:T(2,128)S(1)} %copy-done.2, s32[2,20]{1,0:T(2,128)S(1)} %copy-done.3, ...), custom_call_target="tpu_custom_call" | custom-call | tf_op jit(solution)/shard_map/filter_steps/pallas_call | solution.py:316
  57.4 0.7 %copy.12 = bf16[512,128]{1,0:T(8,128)(2,1)} copy(bf16[512,128]{1,0:T(8,128)(2,1)S(1)} %filter_steps.1) | data formatting | bytes 262144
Async XLA Ops:
  3.5 0.7 %copy-start.3 = (s32[2,20]{1,0:T(2,128)S(1)}, s32[2,20]{1,0:T(2,128)}, u32[]{:S(2)}) copy-start(s32[2,20]{1,0:T(2,128)} %get-tuple-element.8.last_ref) | copy-start | bytes 484
  3.5 0.7 %copy-start.5 = (s32[1,32]{1,0:T(1,128)S(1)}, s32[1,32]{1,0:T(1,128)}, u32[]{:S(2)}) copy-start(s32[1,32]{1,0:T(1,128)} %cols_ref.3) | copy-start | bytes 388
  3.5 0.7 %copy-start.2 = (s32[2,32]{1,0:T(2,128)S(1)}, s32[2,32]{1,0:T(2,128)}, u32[]{:S(2)}) copy-start(s32[2,32]{1,0:T(2,128)} %get-tuple-element.7.prev_ref) | copy-start | bytes 772
  3.5 0.7 %copy-start.4 = (s32[1,32]{1,0:T(1,128)S(1)}, s32[1,32]{1,0:T(1,128)}, u32[]{:S(2)}) copy-start(s32[1,32]{1,0:T(1,128)} %rows_ref.3) | copy-start | bytes 388
  4.2 1.2 %copy-start = (bf16[1,32,128,128]{3,2,1,0:T(8,128)(2,1)S(1)}, bf16[1,32,128,128]{3,2,1,0:T(8,128)(2,1)}, u32[]{:S(2)}) copy-start(bf16[1,32,128,128]{3,2,1,0:T(8,128)(2,1)} %tiles_ref.1) | copy-start | bytes 3145732
  5.4 0.9 %copy-start.1 = (bf16[512,128]{1,0:T(8,128)(2,1)S(1)}, bf16[512,128]{1,0:T(8,128)(2,1)}, u32[]{:S(2)}) copy-start(bf16[512,128]{1,0:T(8,128)(2,1)} %x_ref.1) | copy-start | bytes 393220

commit v5 on v4

--- a/solution.py
+++ b/solution.py
@@ -8,7 +8,7 @@
 from jax.sharding import PartitionSpec as P
 
 CHUNKS = 2
-UNROLL = 8
+UNROLL = 16
 MESH_ID = pl.DeviceIdType.MESH
 
 

time: 58.3 us -> 57.6 us (0.988)
  Pallas kernels: 52.6 us -> 52 us
    pallas_call x1, Pallas kernels: 51 us -> 50.4 us  [per_device(): pl.pallas_call(functools.partial(filter_kernel, (R, C, half, pt, slots, v...]
where the time goes in v5:
time: 57.6 us; the launch traced here: 57.4 us
  Pallas kernels  52 us (90%)
  local copies, waits for them, and re-layouts  3.46 us (6%)
  between operations  1.99 us (3%)
    pallas_call x1, Pallas kernels, per_device(): pl.pallas_call(functools.partial(filter_kernel, (R, C, half, pt, slots, v...  50.4 us
    unnamed x13, local copies, waits for them, and re-layouts  3.46 us
    pallas_call x1, Pallas kernels, per_device(): pl.pallas_call(functools.partial(link_slots, slots=slots, row_tiles=row_t...  1.58 us

profile of v5, /device:TPU:0, one launch (start us, length us, event | category | flops | bytes accessed | tf_op | source)
XLA Modules:
  0.0 57.4 jit_solution(17426468510959127212)
XLA Ops:
  1.9 1.6 %link_slots.1 = (s32[2,32]{1,0:T(2,128)}, s32[2,20]{1,0:T(2,128)}) custom-call(s32[1,32]{1,0:T(1,128)} %rows_ref.3, s32[1,32]{1,0:T(1,128)} %cols_ref.3, s32[1,1]{1,0:T(1,128)S(6)} %copy.9.counts_ref), custom_call_target="tpu_custom_call" | custom-call | tf_op jit(solution)/shard_map/link_slots/pallas_call | solution.py:287
  3.5 0.0 copy-start.3
  3.5 0.0 copy-start.5
  3.6 0.0 copy-start.2
  3.6 0.0 copy-start.4
  3.6 0.6 %copy-done.3 = s32[2,20]{1,0:T(2,128)S(1)} copy-done((s32[2,20]{1,0:T(2,128)S(1)}, s32[2,20]{1,0:T(2,128)}, u32[]{:S(2)}) %copy-start.3) | copy-done | bytes 184
  4.2 0.0 copy-done.5
  4.2 0.0 copy-done.2
  4.2 0.0 copy-done.4
  4.2 0.0 copy-start
  4.2 1.2 %copy-done = bf16[1,32,128,128]{3,2,1,0:T(8,128)(2,1)S(1)} copy-done((bf16[1,32,128,128]{3,2,1,0:T(8,128)(2,1)S(1)}, bf16[1,32,128,128]{3,2,1,0:T(8,128)(2,1)}, u32[]{:S(2)}) %copy-start) | copy-done | bytes 1048600
  5.5 0.0 copy-start.1
  5.5 0.9 %copy-done.1 = bf16[512,128]{1,0:T(8,128)(2,1)S(1)} copy-done((bf16[512,128]{1,0:T(8,128)(2,1)S(1)}, bf16[512,128]{1,0:T(8,128)(2,1)}, u32[]{:S(2)}) %copy-start.1) | copy-done | bytes 131096
  6.4 50.4 %filter_steps.1 = bf16[512,128]{1,0:T(8,128)(2,1)S(1)} custom-call(bf16[512,128]{1,0:T(8,128)(2,1)S(1)} %copy-done.1, bf16[1,32,128,128]{3,2,1,0:T(8,128)(2,1)S(1)} %copy-done, s32[1,32]{1,0:T(1,128)S(1)} %copy-done.4, s32[1,32]{1,0:T(1,128)S(1)} %copy-done.5, s32[2,32]{1,0:T(2,128)S(1)} %copy-done.2, s32[2,20]{1,0:T(2,128)S(1)} %copy-done.3, ...), custom_call_target="tpu_custom_call" | custom-call | tf_op jit(solution)/shard_map/filter_steps/pallas_call | solution.py:316
  56.8 0.7 %copy.12 = bf16[512,128]{1,0:T(8,128)(2,1)} copy(bf16[512,128]{1,0:T(8,128)(2,1)S(1)} %filter_steps.1) | data formatting | bytes 262144
Async XLA Ops:
  3.5 0.7 %copy-start.3 = (s32[2,20]{1,0:T(2,128)S(1)}, s32[2,20]{1,0:T(2,128)}, u32[]{:S(2)}) copy-start(s32[2,20]{1,0:T(2,128)} %get-tuple-element.8.last_ref) | copy-start | bytes 484
  3.5 0.7 %copy-start.5 = (s32[1,32]{1,0:T(1,128)S(1)}, s32[1,32]{1,0:T(1,128)}, u32[]{:S(2)}) copy-start(s32[1,32]{1,0:T(1,128)} %cols_ref.3) | copy-start | bytes 388
  3.6 0.7 %copy-start.2 = (s32[2,32]{1,0:T(2,128)S(1)}, s32[2,32]{1,0:T(2,128)}, u32[]{:S(2)}) copy-start(s32[2,32]{1,0:T(2,128)} %get-tuple-element.7.prev_ref) | copy-start | bytes 772
  3.6 0.7 %copy-start.4 = (s32[1,32]{1,0:T(1,128)S(1)}, s32[1,32]{1,0:T(1,128)}, u32[]{:S(2)}) copy-start(s32[1,32]{1,0:T(1,128)} %rows_ref.3) | copy-start | bytes 388
  4.2 1.2 %copy-start = (bf16[1,32,128,128]{3,2,1,0:T(8,128)(2,1)S(1)}, bf16[1,32,128,128]{3,2,1,0:T(8,128)(2,1)}, u32[]{:S(2)}) copy-start(bf16[1,32,128,128]{3,2,1,0:T(8,128)(2,1)} %tiles_ref.1) | copy-start | bytes 3145732
  5.5 0.9 %copy-start.1 = (bf16[512,128]{1,0:T(8,128)(2,1)S(1)}, bf16[512,128]{1,0:T(8,128)(2,1)}, u32[]{:S(2)}) copy-start(bf16[512,128]{1,0:T(8,128)(2,1)} %x_ref.1) | copy-start | bytes 393220
